TPU v7x, 32 devices: a whole 2x2x4 slice. The times are simulated.
32 devices in a mesh: dp: 16 (over z, x, core), tensor: 2 (over y).
Axes of the slice: x: 2, y: 2, z: 4, core: 2. Of those that a mesh axis runs over, the one named last changes fastest.
Arguments:
- inputs: bfloat16 [16, 256, 1024], P('dp'), may hold values from -6 to 6
- cotangent: bfloat16 [16, 256, 1024], P('dp'), may hold values from -6 to 6
- lengths: int32 [16], P('dp'), may hold values from 16 to 256, as said below
- norm1_gain: float32 [1024], replicated, may hold values from 0.5 to 1.5
- w_query: bfloat16 [1024, 1024], P(None, 'tensor'), may hold values from -0.1875 to 0.1875
- w_key: bfloat16 [1024, 1024], P(None, 'tensor'), may hold values from -0.1875 to 0.1875
- w_value: bfloat16 [1024, 2048], P(None, 'tensor'), may hold values from -0.1875 to 0.1875
- w_gate: bfloat16 [1024, 2048], P(None, 'tensor'), may hold values from -0.1875 to 0.1875
- w_alpha: bfloat16 [1024, 8], P(None, 'tensor'), may hold values from -0.1875 to 0.1875
- w_beta: bfloat16 [1024, 8], P(None, 'tensor'), may hold values from -0.1875 to 0.1875
- conv_query: float32 [4, 1024], P(None, 'tensor'), may hold values from -3 to 3
- conv_key: float32 [4, 1024], P(None, 'tensor'), may hold values from -3 to 3
- conv_value: float32 [4, 2048], P(None, 'tensor'), may hold values from -3 to 3
- a_log: float32 [8], P('tensor'), may hold values from -7 to -2.5
- dt_bias: float32 [8], P('tensor'), may hold values from -4 to 1
- onorm_gain: float32 [256], replicated, may hold values from 0.5 to 1.5
- w_out: bfloat16 [2048, 1024], P('tensor'), may hold values from -0.25 to 0.25
- norm2_gain: float32 [1024], replicated, may hold values from 0.5 to 1.5
- w_one: bfloat16 [1024, 2816], P(None, 'tensor'), may hold values from -0.1875 to 0.1875
- w_three: bfloat16 [1024, 2816], P(None, 'tensor'), may hold values from -0.1875 to 0.1875
- w_two: bfloat16 [2816, 1024], P('tensor'), may hold values from -0.15625 to 0.15625
Outputs:
- outputs: float32 [16, 256, 1024], P('dp')
- in_grad: float32 [16, 256, 1024], P('dp')
- grad_norm1_gain: float32 [1024], replicated
- grad_w_query: float32 [1024, 1024], P('dp', 'tensor')
- grad_w_key: float32 [1024, 1024], P('dp', 'tensor')
- grad_w_value: float32 [1024, 2048], P('dp', 'tensor')
- grad_w_gate: float32 [1024, 2048], P('dp', 'tensor')
- grad_w_alpha: float32 [1024, 8], P('dp', 'tensor')
- grad_w_beta: float32 [1024, 8], P('dp', 'tensor')
- grad_conv_query: float32 [4, 1024], P(None, 'tensor')
- grad_conv_key: float32 [4, 1024], P(None, 'tensor')
- grad_conv_value: float32 [4, 2048], P(None, 'tensor')
- grad_a_log: float32 [8], P('tensor')
- grad_dt_bias: float32 [8], P('tensor')
- grad_onorm_gain: float32 [256], replicated
- grad_w_out: float32 [2048, 1024], P('tensor', 'dp')
- grad_norm2_gain: float32 [1024], replicated
- grad_w_one: float32 [1024, 2816], P('dp', 'tensor')
- grad_w_three: float32 [1024, 2816], P('dp', 'tensor')
- grad_w_two: float32 [2816, 1024], P('tensor', 'dp')
Inputs may be any that keep to these rules, and one draw needn't show every extreme that they name: Each slot holds one sequence from position 0; positions from lengths[s] on are padding. Slot 0 always holds a sequence of 256 positions; the slots of one index of dp share a drawn upper limit, so loads differ between devices.
All inputs are finite; a program needn't handle non-finite values.
Results may differ from a plain program's by a relative error of at most 0.02.
Values sent between devices are 32-bit elements; how exact they have to be, the bound alone decides.
No kernel may reach another device: no remote copies, remote signals or barrier semaphores. Data moves between devices by JAX's collectives and lax.ppermute only.
A program may use at most 256 MiB of HBM per device.

v0:
```python
import functools
import math

import jax
import jax.numpy as jnp
from jax import lax
from jax.experimental import pallas as pl
from jax.experimental.pallas import tpu as pltpu
from jax.sharding import PartitionSpec as P


epsilon = 1e-06
DP, TENSOR = "dp", "tensor"
f32 = jnp.float32
bf16 = jnp.bfloat16
CHUNK = 128
PARTS = 2
LANES = 128


def rms_scale(rows_in, gain_in):
    return (
        rows_in * lax.rsqrt(jnp.mean(rows_in * rows_in, axis=-1, keepdims=True) + epsilon) * gain_in
    )


def matmul_nt(first_arr, second_arr):
    return lax.dot_general(
        first_arr, second_arr, (((1,), (1,)), ((), ())), preferred_element_type=f32
    )


def halves(value):
    high = value.astype(bf16)
    return high, (value - high.astype(f32)).astype(bf16)


def mm(first_arr, second_arr, first_dim=1, second_dim=0):
    first = first_arr if isinstance(first_arr, tuple) else halves(first_arr)
    second = second_arr if isinstance(second_arr, tuple) else halves(second_arr)
    dims = (((first_dim,), (second_dim,)), ((), ()))

    def one(lhs, rhs):
        return lax.dot_general(lhs, rhs, dims, preferred_element_type=f32)

    return one(first[0], second[0]) + (one(first[0], second[1]) + one(first[1], second[0]))


def delayed(series, steps):
    if steps == 0:
        return series
    rows = lax.broadcasted_iota(jnp.int32, series.shape, 0)
    return jnp.where(rows >= steps, pltpu.roll(series, steps, 0), 0.0)


def advanced(series, steps):
    if steps == 0:
        return series
    length = series.shape[0]
    rows = lax.broadcasted_iota(jnp.int32, series.shape, 0)
    return jnp.where(rows < length - steps, pltpu.roll(series, length - steps, 0), 0.0)


def conv_of(series, taps):
    count = taps.shape[0]
    total = taps[count - 1 : count] * series
    for tap in range(count - 1):
        total = total + taps[tap : tap + 1] * delayed(series, count - 1 - tap)
    return total


def conv_back(series, taps, cotangent):
    count = taps.shape[0]
    d_series = taps[count - 1 : count] * cotangent
    d_taps = []
    for tap in range(count):
        steps = count - 1 - tap
        if steps > 0:
            d_series = d_series + taps[tap : tap + 1] * advanced(cotangent, steps)
        d_taps.append(jnp.sum(cotangent * delayed(series, steps), axis=0, keepdims=True))
    return d_series, d_taps


def silu_slope(value, sig):
    return sig * (1.0 + value * (1.0 - sig))


def unit_back(act, norm, cotangent, scale):
    inner = jnp.sum(cotangent * act, axis=1, keepdims=True)
    return scale * (norm * cotangent - act * (norm * norm * norm * inner))


class Grid2:
    def __init__(self, length):
        row = lax.broadcasted_iota(jnp.int32, (length, length), 0)
        col = lax.broadcasted_iota(jnp.int32, (length, length), 1)
        self.row, self.col = row, col
        self.lower = row >= col
        self.strict = row > col
        self.upper = row <= col
        self.eye = row == col

    def to_row(self, column):
        return jnp.sum(jnp.where(self.eye, column, 0.0), axis=0, keepdims=True)


def lane_of(values, lane):
    lanes = lax.broadcasted_iota(jnp.int32, values.shape, 1)
    return jnp.sum(jnp.where(lanes == lane, values, 0.0), axis=1, keepdims=True)


class Terms:
    pass


def head_terms(raws, taps, ab, rate, bias, lane, heads, grid2):
    t = Terms()
    t.raw = raws
    t.pre = [conv_of(raw, tap) for raw, tap in zip(raws, taps)]
    t.sig = [jax.nn.sigmoid(pre) for pre in t.pre]
    t.act = [pre * sig for pre, sig in zip(t.pre, t.sig)]
    t.norm = [lax.rsqrt(jnp.sum(act * act, axis=1, keepdims=True) + epsilon) for act in t.act[:2]]
    q = t.act[0] * t.norm[0] * raws[0].shape[1] ** (-0.5)
    k = t.act[1] * t.norm[1]
    t.v = t.act[2]
    t.beta = jax.nn.sigmoid(lane_of(ab, heads + lane))
    z = lane_of(ab, lane) + lane_of(bias, lane)
    t.z = z
    t.rate = -jnp.exp(lane_of(rate, lane))
    t.decay = t.rate * (jnp.maximum(z, 0.0) + jnp.log1p(jnp.exp(-jnp.abs(z))))
    decay_row = grid2.to_row(t.decay)
    cum_col = jnp.sum(jnp.where(grid2.lower, decay_row, 0.0), axis=1, keepdims=True)
    cum_row = jnp.sum(jnp.where(grid2.upper, t.decay, 0.0), axis=0, keepdims=True)
    differ = jnp.where(grid2.lower, cum_col - cum_row, 0.0)
    t.within = jnp.where(grid2.lower, jnp.exp(differ), 0.0)
    t.q2, t.k2 = halves(q), halves(k)
    t.kk = jnp.where(grid2.strict, mm(t.k2, t.k2, 1, 1), 0.0) * t.within
    t.system = t.beta * t.kk
    t.scores = mm(t.q2, t.k2, 1, 1) * t.within
    return t


def unit_lower_inverses(blocks_of, found_ref, count):
    size = found_ref.shape[-1]
    row = lax.broadcasted_iota(jnp.int32, (size, size), 0)
    col = lax.broadcasted_iota(jnp.int32, (size, size), 1)

    def joined(index, level):
        pair = (row >> (level + 1) == col >> (level + 1)) & (row >> level != col >> level)
        return jnp.where(pair, blocks_of(index), 0.0)

    for index in range(count):
        found_ref[0, index] = jnp.where(row == col, 1.0, 0.0) - joined(index, 0)

    def join(level, carry):
        found = [found_ref[0, index] for index in range(count)]
        split = [halves(inv) for inv in found]
        left = [mm(inv, joined(index, level)) for index, inv in enumerate(split)]
        for index in range(count):
            found_ref[0, index] = found[index] - mm(left[index], split[index])
        return carry

    lax.fori_loop(1, size.bit_length() - 1, join, 0)


def forward_kernel(
    heads,
    q_ref,
    k_ref,
    v_ref,
    g_ref,
    ab_ref,
    cq_ref,
    ck_ref,
    cv_ref,
    rate_ref,
    bias_ref,
    gain_ref,
    gated_ref,
    trade_ref,
    inv_ref,
    new_ref,
    out_ref,
    system_ref,
    scores_ref,
):
    length = q_ref.shape[0]
    dv = v_ref.shape[1] // heads
    chunk = min(CHUNK, length)
    blocks = length // chunk
    grid2 = Grid2(length)
    dk = q_ref.shape[1] // heads
    ab, rate, bias = ab_ref[...].astype(f32), rate_ref[...], bias_ref[...]

    def cols_of(h, width):
        return pl.ds(pl.multiple_of(h * width, width), width)

    def begin(h, carry):
        ks, vs = cols_of(h, dk), cols_of(h, dv)
        raws = (q_ref[:, ks].astype(f32), k_ref[:, ks].astype(f32), v_ref[:, vs].astype(f32))
        taps = (cq_ref[:, ks], ck_ref[:, ks], cv_ref[:, vs])
        t = head_terms(raws, taps, ab, rate, bias, h, heads, grid2)
        system_ref[h] = t.system
        scores_ref[h] = t.scores
        new_ref[:, vs] = t.beta * t.v
        return carry

    lax.fori_loop(0, heads, begin, 0)

    def block_of(index):
        at = slice(index % blocks * chunk, (index % blocks + 1) * chunk)
        return system_ref[index // blocks, at, at]

    unit_lower_inverses(block_of, inv_ref, heads * blocks)
    gain = gain_ref[...]

    def finish(h, carry):
        cols = cols_of(h, dv)
        for b in range(blocks):
            rows = slice(b * chunk, (b + 1) * chunk)
            rhs = new_ref[rows, cols]
            if b > 0:
                rhs = rhs - mm(system_ref[h, rows, : b * chunk], new_ref[: b * chunk, cols])
            new_ref[rows, cols] = mm(inv_ref[0, h * blocks + b], rhs)
        out = mm(scores_ref[h], new_ref[:, cols])
        out_ref[:, cols] = out
        scaled = out * lax.rsqrt(jnp.mean(out * out, axis=1, keepdims=True) + epsilon) * gain
        gate = g_ref[:, cols].astype(f32)
        gated = (scaled * (gate * jax.nn.sigmoid(gate))).astype(bf16)
        gated_ref[:, cols] = gated
        trade_ref[:, cols] = gated.astype(f32)
        return carry

    lax.fori_loop(0, heads, finish, 0)


def backward_kernel(first_head, heads, chained, *refs):
    (q_ref, k_ref, v_ref, g_ref, ab_ref, cq_ref, ck_ref, cv_ref, rate_ref, bias_ref, gain_ref) = refs[:11]
    (inv_ref, new_ref, out_ref, d_gated_ref, wq_ref, wk_ref, wv_ref, wg_ref, wab_ref) = refs[11:20]
    refs = refs[20:]
    dh_ref, dab_ref, dsmall_ref, dgain_ref, trade_ref, dcq_ref, dck_ref, dcv_ref = refs[-8:]
    length = q_ref.shape[0]
    dkey = q_ref.shape[1]
    chunk = min(CHUNK, length)
    blocks = length // chunk
    grid2 = Grid2(length)
    seq, head = pl.program_id(0), pl.program_id(1)
    lane = first_head + head

    for ref, index, fresh in (
        (dh_ref, 0, head == 0),
        (dab_ref, 1, head == 0),
        (dsmall_ref, 2, (head == 0) & (seq == 0)),
        (dgain_ref, 3, (head == 0) & (seq == 0)),
    ):

        @pl.when(fresh)
        def _(ref=ref, index=index):
            ref[...] = refs[index][...] if chained else jnp.zeros_like(ref)

    gain = gain_ref[...]
    raws = (q_ref[...].astype(f32), k_ref[...].astype(f32), v_ref[...].astype(f32))
    taps = (cq_ref[...], ck_ref[...], cv_ref[...])
    t = head_terms(raws, taps, ab_ref[...].astype(f32), rate_ref[...], bias_ref[...], lane, heads, grid2)
    q2, k2, v, beta, within = t.q2, t.k2, t.v, t.beta, t.within
    new2, out = halves(new_ref[...]), out_ref[...]
    d_gated = d_gated_ref[...]
    gate = g_ref[...].astype(f32)
    gate_sig = jax.nn.sigmoid(gate)
    norm = lax.rsqrt(jnp.mean(out * out, axis=1, keepdims=True) + epsilon)
    unit = out * norm
    d_gate = (d_gated * unit * gain * silu_slope(gate, gate_sig)).astype(bf16)
    d_scaled = d_gated * (gate * gate_sig)
    dgain_ref[...] += jnp.sum(d_scaled * unit, axis=0, keepdims=True)
    d_unit = d_scaled * gain
    inner = jnp.mean(d_unit * unit, axis=1, keepdims=True)
    d_out2 = halves(norm * (d_unit - unit * inner))
    d_new = mm(t.scores, d_out2, 0, 0)
    d_scores = mm(d_out2, new2, 1, 1)
    solved = [None] * blocks
    for b in reversed(range(blocks)):
        rows = slice(b * chunk, (b + 1) * chunk)
        rhs = d_new[rows]
        for later in range(b + 1, blocks):
            part = t.system[later * chunk : (later + 1) * chunk, rows]
            rhs = rhs - mm(part, solved[later], 0, 0)
        solved[b] = mm(inv_ref[0, b], rhs, 0, 0)
    y = jnp.concatenate(solved, axis=0)
    d_system = jnp.where(grid2.strict, -mm(y, new2, 1, 1), 0.0)
    d_qk2, d_kk2 = halves(d_scores * within), halves(beta * d_system * within)
    d_beta = jnp.sum(y * v, axis=1, keepdims=True) + jnp.sum(d_system * t.kk, axis=1, keepdims=True)
    flow = d_system * t.system + d_scores * t.scores
    d_cum = grid2.to_row(jnp.sum(flow, axis=1, keepdims=True)) - jnp.sum(flow, axis=0, keepdims=True)
    d_decay = jnp.sum(jnp.where(grid2.upper, d_cum, 0.0), axis=1, keepdims=True)
    d_z = d_decay * t.rate * jax.nn.sigmoid(t.z)
    d_b = d_beta * beta * (1.0 - beta)
    d_rate = jnp.sum(d_decay * t.decay, axis=0, keepdims=True)
    d_bias = jnp.sum(d_z, axis=0, keepdims=True)
    small_row = lax.broadcasted_iota(jnp.int32, dsmall_ref.shape, 0)
    small_lane = lax.broadcasted_iota(jnp.int32, dsmall_ref.shape, 1)
    dsmall_ref[...] += jnp.where((small_row == 0) & (small_lane == lane), d_rate, 0.0) + jnp.where(
        (small_row == 1) & (small_lane == lane), d_bias, 0.0
    )
    ab_lane = lax.broadcasted_iota(jnp.int32, dab_ref.shape, 1)
    d_z, d_b = d_z.astype(bf16).astype(f32), d_b.astype(bf16).astype(f32)
    dab_ref[...] += jnp.where(ab_lane == lane, d_z, 0.0) + jnp.where(ab_lane == heads + lane, d_b, 0.0)
    d_q = mm(d_qk2, k2)
    d_k = mm(d_qk2, q2, 0, 0) + mm(d_kk2, k2) + mm(d_kk2, k2, 0, 0)
    d_q = unit_back(t.act[0], t.norm[0], d_q, dkey ** (-0.5))
    d_k = unit_back(t.act[1], t.norm[1], d_k, 1.0)
    d_raws = []
    d_acts, d_conv_refs = (d_q, d_k, beta * y), (dcq_ref, dck_ref, dcv_ref)
    for cot, pre, sig, raw, tap, d_conv_ref in zip(d_acts, t.pre, t.sig, t.raw, taps, d_conv_refs):
        d_raw, d_taps = conv_back(raw, tap, cot * silu_slope(pre, sig))
        d_raws.append(d_raw.astype(bf16))
        for index, d_tap in enumerate(d_taps):
            d_conv_ref[0, index : index + 1, :] = d_tap
    d_raws.append(d_gate)
    d_h = d_z * wab_ref[pl.ds(lane, 1), :] + d_b * wab_ref[pl.ds(heads + lane, 1), :]
    start = 0
    for d_raw, w_ref in zip(d_raws, (wq_ref, wk_ref, wv_ref, wg_ref)):
        d_h = d_h + matmul_nt(d_raw, w_ref[...])
        trade_ref[:, start : start + d_raw.shape[1]] = d_raw.astype(f32)
        start += d_raw.shape[1]
    dh_ref[...] += d_h


def whole(shape):
    return pl.BlockSpec(shape, lambda s: (0,) * len(shape))


def by_seq(length, cols):
    return pl.BlockSpec((length, cols), lambda s: (s, 0))


def mixer_specs(length, arrays):
    q, k, v, g, ab, cq, ck, cv, rate, bias, gain = arrays
    return [by_seq(length, arr.shape[1]) for arr in (q, k, v, g, ab)] + [
        whole(arr.shape) for arr in (cq, ck, cv, rate, bias, gain)
    ]


def mixer_forward(heads, length, arrays):
    rows = arrays[0].shape[0]
    seqs = rows // length
    wide = arrays[2].shape[1]
    chunk = min(CHUNK, length)
    count = heads * (length // chunk)
    return pl.pallas_call(
        functools.partial(forward_kernel, heads),
        grid=(seqs,),
        in_specs=mixer_specs(length, arrays),
        out_specs=[
            by_seq(length, wide),
            by_seq(length, wide),
            pl.BlockSpec((1, count, chunk, chunk), lambda s: (s, 0, 0, 0)),
            by_seq(length, wide),
            by_seq(length, wide),
        ],
        out_shape=[
            jax.ShapeDtypeStruct((rows, wide), bf16),
            jax.ShapeDtypeStruct((rows, wide), f32),
            jax.ShapeDtypeStruct((seqs, count, chunk, chunk), f32),
            jax.ShapeDtypeStruct((rows, wide), f32),
            jax.ShapeDtypeStruct((rows, wide), f32),
        ],
        scratch_shapes=[
            pltpu.VMEM((heads, length, length), f32),
            pltpu.VMEM((heads, length, length), f32),
        ],
        name="forward",
    )(*arrays)


def mixer_backward(part, parts, heads, length, arrays, saved, d_gated, weights, before):
    rows = arrays[0].shape[0]
    seqs = rows // length
    q, _, v, _, ab, cq, ck, cv, rate, bias, gain = arrays
    inv, new, out = saved
    chunk = min(CHUNK, length)
    count = length // chunk
    own = heads // parts
    first = part * own
    width_d = weights[0].shape[0]
    dkey, dval = q.shape[1] // heads, v.shape[1] // heads
    trade = 2 * (dkey + dval)

    def seq_spec(cols):
        return pl.BlockSpec((length, cols), lambda s, h: (s, first + h))

    def col_spec(arr):
        return pl.BlockSpec((arr.shape[0], arr.shape[1] // heads), lambda s, h: (0, first + h))

    def fixed(shape):
        return pl.BlockSpec(shape, lambda s, h: (0,) * len(shape))

    def per_seq(cols):
        return pl.BlockSpec((length, cols), lambda s, h: (s, 0))

    sums = [
        (per_seq(width_d), jax.ShapeDtypeStruct((rows, width_d), f32)),
        (per_seq(ab.shape[1]), jax.ShapeDtypeStruct(ab.shape, f32)),
        (fixed((8, LANES)), jax.ShapeDtypeStruct((8, LANES), f32)),
        (fixed(gain.shape), jax.ShapeDtypeStruct(gain.shape, f32)),
    ]

    def conv_out(arr):
        cols = arr.shape[1]
        return (
            pl.BlockSpec((1, arr.shape[0], cols // heads), lambda s, h: (s, 0, h)),
            jax.ShapeDtypeStruct((seqs, arr.shape[0], cols // parts), f32),
        )

    outs = sums + [
        (
            pl.BlockSpec((length, trade), lambda s, h: (s, h)),
            jax.ShapeDtypeStruct((rows, trade * own), f32),
        )
    ]
    outs += [conv_out(arr) for arr in (cq, ck, cv)]
    before = list(before or ())
    return pl.pallas_call(
        functools.partial(backward_kernel, first, heads, bool(before)),
        grid=(seqs, own),
        in_specs=[seq_spec(dkey), seq_spec(dkey), seq_spec(dval), seq_spec(dval), per_seq(ab.shape[1])]
        + [col_spec(arr) for arr in (cq, ck, cv)]
        + [fixed(arr.shape) for arr in (rate, bias, gain)]
        + [pl.BlockSpec((1, count, chunk, chunk), lambda s, h: (s, first + h, 0, 0))]
        + [seq_spec(dval)] * 3
        + [col_spec(arr) for arr in weights[:4]]
        + [fixed(weights[4].shape)]
        + [spec for spec, _ in sums[: len(before)]],
        out_specs=[spec for spec, _ in outs],
        out_shape=[shape for _, shape in outs],
    )(*arrays, inv, new, out, d_gated, *weights, *before)


def swap(value, axis):
    size = lax.axis_size(axis)
    if size == 1:
        return jnp.zeros_like(value)
    return lax.ppermute(value, axis, [(i, i ^ 1) for i in range(size)])


def sum_over(value, axis):
    size = lax.axis_size(axis)
    if size & (size - 1):
        return lax.psum(value, axis)
    step = 1
    while step < size:
        other = lax.ppermute(value, axis, [(i, i ^ step) for i in range(size)])
        value = value + other
        step *= 2
    return value


def ring_order(count):
    return list(range(0, count, 2)) + list(range(1, count, 2))[::-1]


class Ring:
    def __init__(self, axis, width):
        self.axis = axis
        size = lax.axis_size(axis)
        self.count = size // 2
        order = ring_order(self.count)
        place = [order.index(chip) for chip in range(self.count)]
        me = lax.axis_index(axis)
        core = me % 2
        pos = jnp.asarray(place, jnp.int32)[me // 2]
        self.up = [(order[p] * 2 + c, order[(p + 1) % self.count] * 2 + c) for p in range(self.count) for c in (0, 1)]
        self.down = [(dst, src) for src, dst in self.up]
        self.block = width // size
        row = lax.broadcasted_iota(jnp.int32, (self.count, self.block, width), 0)
        off = lax.broadcasted_iota(jnp.int32, (self.count, self.block, width), 1)
        col = lax.broadcasted_iota(jnp.int32, (self.count, self.block, width), 2)
        self.firsts = sorted({0, max(self.count - 2, 0)})
        self.blocks = self.firsts + [m for m in range(self.count) if m not in self.firsts]
        turn = jnp.asarray(self.blocks, jnp.int32)
        chips = jnp.asarray(order, jnp.int32)[(pos - 1 - turn) % self.count]
        start = chips[:, None, None] * (2 * self.block) + off
        shape = (self.count * self.block, width)
        self.mine = (col == start + core * self.block).astype(bf16).reshape(shape)
        self.other = (col == start + (1 - core) * self.block).astype(bf16).reshape(shape)

    def rows(self, source):
        own = matmul_nt(self.mine, source).astype(bf16)
        sent = swap(matmul_nt(self.other, source), self.axis)
        return own, sent

    def reduce(self, partials):
        n, half = self.count, self.block // 2
        where = {}
        for arr in partials:
            for row in range(0, arr.shape[0], self.block):
                where[self.blocks[len(where)]] = (arr, row)

        def part(m, way):
            arr, row = where[m]
            return arr[row + way * half : row + (way + 1) * half]

        if n == 1:
            return partials[0]
        going, coming = part(0, 0), part(n - 2, 1)
        for step in range(n - 1):
            going = lax.ppermute(going, self.axis, self.up)
            coming = lax.ppermute(coming, self.axis, self.down)
            going = going + part(step + 1, 0)
            coming = coming + part((n - 3 - step) % n, 1)
        return jnp.concatenate([going, coming], axis=0)


def grads_kernel(row_of, starts, counts, *refs):
    pairs = max(row_of) + 1
    row_refs, refs = refs[: 2 * pairs], refs[2 * pairs :]
    own_refs, sent_refs = refs[: len(row_of)], refs[len(row_of) : -3]
    out_ref, rows_ref, cols_ref = refs[-3:]
    step = pl.program_id(0)
    depth = row_refs[0].shape[1]

    @pl.when(step == 0)
    def _():
        for pair in range(pairs):
            rows_ref[pair, :, :depth] = row_refs[2 * pair][...]
            rows_ref[pair, :, depth:] = row_refs[2 * pair + 1][...].astype(bf16)

    chosen = 0
    for index, pair in enumerate(row_of):
        here = (step >= starts[index]) & (step < starts[index] + counts[index])
        chosen = chosen + jnp.where(here, pair, 0)

        @pl.when(here)
        def _(index=index):
            cols_ref[:depth] = own_refs[index][...].astype(bf16)
            cols_ref[depth:] = sent_refs[index][...].astype(bf16)

    out_ref[...] = jnp.dot(rows_ref[chosen], cols_ref[...], preferred_element_type=f32)


def weight_grads(rows, cols, height):
    widths = [width for *_, width in cols]
    tile = math.gcd(*widths, *[first for *_, first, _ in cols])
    tile = 512 if tile % 512 == 0 else tile
    counts = [width // tile for width in widths]
    starts = [sum(counts[:i]) for i in range(len(counts))]
    flat_rows = [arr for pair in rows for arr in pair]
    depth = flat_rows[0].shape[1]

    def col_spec(start, span, first):
        return pl.BlockSpec((depth, tile), lambda j: (0, first + jnp.clip(j - start, 0, span - 1)))

    firsts = [first // tile for *_, first, _ in cols]
    col_specs = [col_spec(*places) for places in zip(starts, counts, firsts)]
    return pl.pallas_call(
        functools.partial(grads_kernel, tuple(pair for pair, *_ in cols), tuple(starts), tuple(counts)),
        grid=(sum(counts),),
        in_specs=[pl.BlockSpec((height, depth), lambda j: (0, 0)) for _ in flat_rows] + col_specs * 2,
        out_specs=pl.BlockSpec((height, tile), lambda j: (0, j)),
        out_shape=jax.ShapeDtypeStruct((height, sum(widths)), f32),
        scratch_shapes=[
            pltpu.VMEM((len(rows), height, 2 * depth), bf16),
            pltpu.VMEM((2 * depth, tile), bf16),
        ],
    )(*flat_rows, *[col[1] for col in cols], *[col[2] for col in cols])


def layer(
    inputs,
    cotangent,
    lengths,
    norm1_gain,
    w_query,
    w_key,
    w_value,
    w_gate,
    w_alpha,
    w_beta,
    conv_query,
    conv_key,
    conv_value,
    a_log,
    dt_bias,
    onorm_gain,
    w_out,
    norm2_gain,
    w_one,
    w_three,
    w_two,
):
    seq_count, seq_len, width_d = inputs.shape
    row_count = seq_count * seq_len
    heads = a_log.shape[0]
    ring = Ring(DP, width_d)

    positions = lax.broadcasted_iota(jnp.int32, (seq_count, seq_len), 1)
    live_rows = (positions < lengths[:, None]).astype(f32).reshape(row_count, 1)
    x_rows = inputs.reshape(row_count, width_d).astype(f32)
    h_one = rms_scale(x_rows, norm1_gain).astype(bf16)
    w_ab = jnp.concatenate([w_alpha, w_beta], axis=1)
    matrices = (w_query, w_key, w_value, w_gate, w_ab)
    raws = tuple(
        jnp.dot(h_one, matrix, preferred_element_type=f32).astype(bf16) for matrix in matrices
    )
    arrays = raws + (
        conv_query,
        conv_key,
        conv_value,
        a_log.reshape(1, heads),
        dt_bias.reshape(1, heads),
        onorm_gain.reshape(1, -1),
    )
    gated_out, gated_trade, *saved = mixer_forward(heads, seq_len, arrays)
    mixed = jnp.dot(gated_out, w_out, preferred_element_type=f32)
    x_mid = x_rows + (mixed + swap(mixed, TENSOR))

    grad_out = cotangent.reshape(row_count, width_d).astype(f32) * live_rows
    grad_out_b = grad_out.astype(bf16)
    d_hidden = matmul_nt(grad_out_b, w_two)
    rows_out = ring.rows(grad_out_b)
    rows_one = ring.rows(h_one)
    gated_sent = swap(gated_trade, DP)

    h_two = rms_scale(x_mid, norm2_gain).astype(bf16)
    pre_one = jnp.dot(h_two, w_one, preferred_element_type=f32)
    pre_three = jnp.dot(h_two, w_three, preferred_element_type=f32)
    sig_one = jax.nn.sigmoid(pre_one)
    hidden = (pre_one * sig_one * pre_three).astype(bf16)
    d_pre_one = (d_hidden * pre_three * sig_one * (1.0 + pre_one * (1.0 - sig_one))).astype(bf16)
    d_pre_three = (d_hidden * pre_one * sig_one).astype(bf16)
    d_h_two = matmul_nt(d_pre_one, w_one) + matmul_nt(d_pre_three, w_three)
    d_h_two = d_h_two + swap(d_h_two, TENSOR)

    rows_two = ring.rows(h_two)
    ffn_cols = (d_pre_one, d_pre_three, hidden)
    ffn_sent = [swap(arr.astype(f32), DP) for arr in ffn_cols]
    tall = rows_two[0].shape[0]
    ffn_grads = [(pair, own, sent, 0, own.shape[1]) for pair, own, sent in zip((0, 0, 1), ffn_cols, ffn_sent)]
    ffn_partial = weight_grads((rows_two, rows_out), ffn_grads, tall)
    ffn_sum = ring.reduce([ffn_partial])

    ffn_out = jnp.dot(hidden, w_two, preferred_element_type=f32)
    ffn_other = swap(ffn_out, TENSOR)

    _, norm2_back = jax.vjp(rms_scale, x_mid, norm2_gain)
    d_mid_part, grad_norm2 = norm2_back(d_h_two)
    d_x_mid = grad_out + d_mid_part
    d_mid_b = d_x_mid.astype(bf16)
    d_gated = matmul_nt(d_mid_b, w_out)
    rows_mid = ring.rows(d_mid_b)
    weights = (*matrices[:4], jnp.transpose(w_ab).astype(f32))
    sums, trades, convs = None, [], []
    for part in range(PARTS):
        back = mixer_backward(part, PARTS, heads, seq_len, arrays, saved, d_gated, weights, sums)
        sums = back[:4]
        trades.append((back[4], swap(back[4], DP)))
        convs.append([jnp.sum(conv, axis=0) for conv in back[5:]])
    d_h_part, d_ab, g_small, g_onorm = sums

    x_late, ffn_late, d_ab = lax.optimization_barrier((x_mid, ffn_out, d_ab))
    outputs = ((x_late + (ffn_late + ffn_other)) * live_rows).reshape(seq_count, seq_len, width_d)

    d_h_one = d_h_part + swap(d_h_part, TENSOR)
    g_onorm = g_onorm + swap(g_onorm, TENSOR)
    _, norm1_back = jax.vjp(rms_scale, x_rows, norm1_gain)
    d_in_part, grad_norm1 = norm1_back(d_h_one)
    in_grad = (d_x_mid + d_in_part).reshape(seq_count, seq_len, width_d)

    wide = gated_out.shape[1] // PARTS
    mixer_sums = []
    for part, (own, sent) in enumerate(trades):
        cols = [(0, own, sent, 0, own.shape[1]), (1, gated_out, gated_sent, part * wide, wide)]
        partial = weight_grads((rows_one, rows_mid), cols, tall)
        mixer_sums.append(ring.reduce([partial]))

    g_ab = lax.dot_general(d_ab.astype(bf16), h_one, (((0,), (0,)), ((), ())), preferred_element_type=f32)
    g_convs = [conv for part in convs for conv in part]
    small_parts = (grad_norm1, grad_norm2, g_onorm, g_small, g_ab, *g_convs)
    sizes = [part.size // LANES for part in small_parts]
    packed = jnp.concatenate([part.reshape(-1, LANES) for part in small_parts], axis=0)
    packed = sum_over(packed, DP)
    unpacked, offset = [], 0
    for part, size in zip(small_parts, sizes):
        unpacked.append(packed[offset : offset + size].reshape(part.shape))
        offset = offset + size
    grad_norm1, grad_norm2, g_onorm, g_small, g_ab = unpacked[:5]
    g_conv_q, g_conv_k, g_conv_v = (jnp.concatenate(unpacked[5 + i :: 3], axis=1) for i in range(3))
    block = width_d // lax.axis_size(DP)
    g_ab = lax.dynamic_slice_in_dim(g_ab, lax.axis_index(DP) * block, block, axis=1).T

    sizes = [matrix.shape[1] // heads for matrix in matrices[:4]]
    span = sum(sizes)
    heads_end = heads // PARTS * span
    pieces = []
    for index, size in enumerate(sizes):
        start = sum(sizes[:index])
        cols = [total[:, at + start : at + start + size] for total in mixer_sums for at in range(0, heads_end, span)]
        pieces.append(jnp.concatenate(cols, axis=1))
    pieces.append(jnp.concatenate([total[:, heads_end:] for total in mixer_sums], axis=1))
    ff_local = w_one.shape[1]
    return (
        outputs,
        in_grad,
        grad_norm1,
        pieces[0],
        pieces[1],
        pieces[2],
        pieces[3],
        g_ab[:, :heads],
        g_ab[:, heads:],
        g_conv_q,
        g_conv_k,
        g_conv_v,
        g_small[0, :heads],
        g_small[1, :heads],
        g_onorm.reshape(-1),
        jnp.transpose(pieces[4]),
        grad_norm2,
        ffn_sum[:, :ff_local],
        ffn_sum[:, ff_local : 2 * ff_local],
        jnp.transpose(ffn_sum[:, 2 * ff_local :]),
    )


def solution(mesh):
    in_specs = (
        P(DP, None, None),
        P(DP, None, None),
        P(DP),
        P(),
        P(None, TENSOR),
        P(None, TENSOR),
        P(None, TENSOR),
        P(None, TENSOR),
        P(None, TENSOR),
        P(None, TENSOR),
        P(None, TENSOR),
        P(None, TENSOR),
        P(None, TENSOR),
        P(TENSOR),
        P(TENSOR),
        P(),
        P(TENSOR, None),
        P(),
        P(None, TENSOR),
        P(None, TENSOR),
        P(TENSOR, None),
    )
    out_specs = (
        P(DP, None, None),
        P(DP, None, None),
        P(),
        P(DP, TENSOR),
        P(DP, TENSOR),
        P(DP, TENSOR),
        P(DP, TENSOR),
        P(DP, TENSOR),
        P(DP, TENSOR),
        P(None, TENSOR),
        P(None, TENSOR),
        P(None, TENSOR),
        P(TENSOR),
        P(TENSOR),
        P(),
        P(TENSOR, DP),
        P(),
        P(DP, TENSOR),
        P(DP, TENSOR),
        P(TENSOR, DP),
    )
    return jax.shard_map(layer, mesh=mesh, in_specs=in_specs, out_specs=out_specs, check_vma=False)
```

profile of v0, /device:TPU:0, one launch (start us, length us, event | category | flops | bytes accessed | tf_op | source)
XLA Modules:
  0.0 338.6 jit_solution(4638749930117916860)
XLA Ops:
  2.1 2.7 convolution_convert_fusion.3.q_ref.refs_0_
  6.1 1.5 convolution_convert_fusion.1.v_ref.refs_2_
  7.6 1.6 convolution_convert_fusion.g_ref.refs_3_
  10.2 13.7 %forward.1 = (bf16[256,1024]{1,0:T(8,128)(2,1)}, f32[256,1024]{1,0:T(8,128)}, f32[1,8,128,128]{3,2,1,0:T(8,128)}, f32[256,1024]{1,0:T(8,128)}, f32[256,1024]{1,0:T(8,128)}) custom-call(bf16[256,512]{1,0:T(8,128)(2,1)} %convolution_convert_fusion.3.q_ref.refs_0_, bf16[256,512]{1,0:T(8,128)(2,1)} %convolution_convert_fusion.2.k_ref.refs_1_, ...), custom_call_target="tpu_custom_call" | custom-call | tf_op jit(solution)/shard_map/forward/pallas_call | solution.py:349
  24.0 3.5 %fusion.91 = f32[256,1024]{1,0:T(8,128)} fusion(bf16[256,1024]{1,0:T(8,128)(2,1)} %get-tuple-element.44.refs_5_, bf16[1024,1024]{1,0:T(8,128)(2,1)} %param.40), kind=kOutput, calls=%fused_computation.206 | convolution fusion | flops 536870912 | bytes 3670016 | tf_op jit(solution)/shard_map/dot_general | solution.py:613
  27.5 3.0 collective-permute-start
  35.4 2.4 fusion.50
  38.5 2.6 convolution_convert_fusion.5.refs_0_
  41.2 2.5 fusion.53
  44.7 9.3 %collective-permute-done = f32[256,1024]{1,0:T(8,128)} collective-permute-done((f32[256,1024]{1,0:T(8,128)}, f32[256,1024]{1,0:T(8,128)}, u32[]{:S(2)}, u32[]{:S(2)}) %collective-permute-start) | collective-permute-done | bytes 1048608 | tf_op jit(solution)/shard_map/ppermute | solution.py:442
  53.9 1.8 multiply_reduce_fusion.2
  57.0 3.6 %fusion.83 = (f32[256,1408]{1,0:T(8,128)}, bf16[256,1408]{1,0:T(8,128)(2,1)S(1)}, f32[256,1408]{1,0:T(8,128)}, bf16[256,1408]{1,0:T(8,128)(2,1)S(1)}, f32[256,1408]{1,0:T(8,128)}, /*index=5*/bf16[256,1408]{1,0:T(8,128)(2,1)S(1)}) fusion(f32[256,1408]{1,0:T(8,128)S(1)} %fusion.30, f32[256,1408]{1,0:T(8,128)S(1)} %fusion.92, ...), kind=kOutput, calls=%fused_computation.199 | convolution fusion | flops 745046016 | bytes 12779520 | tf_op jit(solution)/shard_map/dot_general | solution.py:624
  62.6 1.8 collective-permute-start.1
  65.7 2.0 fusion.93
  71.1 17.7 %collective-permute-done.1 = f32[256,1024]{1,0:T(8,128)S(1)} collective-permute-done((f32[256,1024]{1,0:T(8,128)S(1)}, f32[256,1024]{1,0:T(8,128)S(1)}, u32[]{:S(2)}, u32[]{:S(2)}) %collective-permute-start.1) | collective-permute-done | bytes 1048608 | tf_op jit(solution)/shard_map/ppermute | solution.py:442
  90.8 1.8 fusion.74.refs_14_
  92.6 10.3 %shard_map.383 = (f32[256,1024]{1,0:T(8,128)}, f32[256,8]{1,0:T(8,128)}, f32[8,128]{1,0:T(8,128)}, f32[1,256]{1,0:T(1,128)}, f32[256,1536]{1,0:T(8,128)}, /*inde...) custom-call(bf16[256,512]{1,0:T(8,128)(2,1)} %convolution_convert_fusion.3.q_ref.refs_0_, ...), custom_call_target="tpu_custom_call" | custom-call | tf_op jit(solution)/shard_map/pallas_call | solution.py:422
  103.0 10.6 %shard_map.384 = (f32[256,1024]{1,0:T(8,128)}, f32[256,8]{1,0:T(8,128)}, f32[8,128]{1,0:T(8,128)}, f32[1,256]{1,0:T(1,128)}, f32[256,1536]{1,0:T(8,128)}, /*inde...) custom-call(bf16[256,512]{1,0:T(8,128)(2,1)} %convolution_convert_fusion.3.q_ref.refs_0_, ...), custom_call_target="tpu_custom_call" | custom-call | tf_op jit(solution)/shard_map/pallas_call | solution.py:422
  115.5 2.7 multiply_bitcast_fusion
  118.2 1.8 collective-permute-start.3
  120.3 8.9 %shard_map.387 = f32[512,4224]{1,0:T(8,128)} custom-call(bf16[512,256]{1,0:T(8,128)(2,1)} %fusion.12.refs_0_, f32[512,256]{1,0:T(8,128)} %collective-permute-done.42.refs_1_, bf16[512,256]{1,0:T(8,128)(2,1)} %convolution_convert_fusion.4.refs_2_, f32[512,256]{1,0:T(8,128)} %collective-permute-done.43.refs_3_, bf16[256,1408]{1,0:T(8,128)(2,1)} %copy-done.19, ...), custom_call_target="tpu_custom_call" | custom-call | tf_op jit(solution)/shard_map/pallas_call | solution.py:554
  129.2 2.3 fusion.86
  131.6 1.7 collective-permute-start.54
  134.0 10.0 %collective-permute-done.4 = f32[1,256]{1,0:T(1,128)S(1)} collective-permute-done((f32[1,256]{1,0:T(1,128)S(1)}, f32[1,256]{1,0:T(1,128)S(1)}, u32[]{:S(2)}, u32[]{:S(2)}) %collective-permute-start.4) | collective-permute-done | bytes 1056 | tf_op jit(solution)/shard_map/ppermute | solution.py:442
  144.1 2.0 fusion.14
  148.8 1.8 collective-permute-start.6
  150.6 2.6 slice_add_fusion.6
  153.7 1.8 collective-permute-start.7
  155.5 14.0 %collective-permute-done.7 = f32[154,128]{1,0:T(8,128)S(1)} collective-permute-done((f32[154,128]{1,0:T(8,128)S(1)}, f32[154,128]{1,0:T(8,128)S(1)}, u32[]{:S(2)}, u32[]{:S(2)}) %collective-permute-start.7) | collective-permute-done | bytes 78880 | tf_op jit(solution)/shard_map/ppermute | solution.py:451
  169.5 2.8 collective-permute-start.8
  172.4 2.8 fusion.24
  178.9 9.9 %collective-permute-done.48 = f32[32,4224]{1,0:T(8,128)S(1)} collective-permute-done((f32[32,4224]{1,0:T(8,128)}, f32[32,4224]{1,0:T(8,128)S(1)}, u32[]{:S(2)}, u32[]{:S(2)}) %collective-permute-start.48) | collective-permute-done | bytes 540704 | tf_op jit(solution)/shard_map/ppermute | solution.py:506
  189.7 2.5 slice_add_fusion.5
  192.2 2.0 collective-permute-start.49
  195.0 6.6 %shard_map.386 = f32[512,2048]{1,0:T(8,128)} custom-call(bf16[512,256]{1,0:T(8,128)(2,1)} %convolution_convert_fusion.5.refs_0_, f32[512,256]{1,0:T(8,128)} %copy-done.16, bf16[512,256]{1,0:T(8,128)(2,1)} %fusion.11.refs_2_, f32[512,256]{1,0:T(8,128)} %copy-done.17, f32[256,1536]{1,0:T(8,128)} %get-tuple-element.67.refs_4_, ...), custom_call_target="tpu_custom_call" | custom-call | tf_op jit(solution)/shard_map/pallas_call | solution.py:554
  203.0 1.6 collective-permute-start.35
  204.7 6.6 %shard_map.385 = f32[512,2048]{1,0:T(8,128)} custom-call(bf16[512,256]{1,0:T(8,128)(2,1)} %convolution_convert_fusion.5.refs_0_, f32[512,256]{1,0:T(8,128)} %copy-done.16, bf16[512,256]{1,0:T(8,128)(2,1)} %fusion.11.refs_2_, f32[512,256]{1,0:T(8,128)} %copy-done.17, f32[256,1536]{1,0:T(8,128)} %get-tuple-element.65.refs_4_, ...), custom_call_target="tpu_custom_call" | custom-call | tf_op jit(solution)/shard_map/pallas_call | solution.py:554
  213.0 1.6 collective-permute-start.20
  216.1 5.6 %collective-permute-done.13 = f32[32,2048]{1,0:T(8,128)S(1)} collective-permute-done((f32[32,2048]{1,0:T(8,128)S(1)}, f32[32,2048]{1,0:T(8,128)S(1)}, u32[]{:S(2)}, u32[]{:S(2)}) %collective-permute-start.13) | collective-permute-done | bytes 262176 | tf_op jit(solution)/shard_map/ppermute | solution.py:506
  223.0 2.0 collective-permute-start.14
  225.0 1.8 slice_add_fusion.4
  226.8 1.6 collective-permute-start.57
  228.9 2.0 collective-permute-done.36
  233.9 2.6 collective-permute-done.21
  237.1 13.1 %collective-permute-done.30 = f32[32,2048]{1,0:T(8,128)S(1)} collective-permute-done((f32[32,2048]{1,0:T(8,128)S(1)}, f32[32,2048]{1,0:T(8,128)S(1)}, u32[]{:S(2)}, u32[]{:S(2)}) %collective-permute-start.30) | collective-permute-done | bytes 262176 | tf_op jit(solution)/shard_map/ppermute | solution.py:506
  252.3 3.5 %collective-permute-done.15 = f32[32,2048]{1,0:T(8,128)S(1)} collective-permute-done((f32[32,2048]{1,0:T(8,128)S(1)}, f32[32,2048]{1,0:T(8,128)S(1)}, u32[]{:S(2)}, u32[]{:S(2)}) %collective-permute-start.15) | collective-permute-done | bytes 262176 | tf_op jit(solution)/shard_map/ppermute | solution.py:506
  257.8 2.1 collective-permute-start.16
  261.3 1.8 collective-permute-start.58
  263.4 1.6 collective-permute-done.38
  267.1 1.7 collective-permute-start.39
  268.7 1.9 collective-permute-done.23
  271.9 12.4 %collective-permute-done.32 = f32[32,2048]{1,0:T(8,128)S(1)} collective-permute-done((f32[32,2048]{1,0:T(8,128)S(1)}, f32[32,2048]{1,0:T(8,128)S(1)}, u32[]{:S(2)}, u32[]{:S(2)}) %collective-permute-start.32) | collective-permute-done | bytes 262176 | tf_op jit(solution)/shard_map/ppermute | solution.py:506
  284.3 1.6 collective-permute-start.24
  286.3 2.2 collective-permute-start.33
  289.9 1.6 collective-permute-start.40
  292.5 3.0 collective-permute-start.18
  296.8 1.6 collective-permute-start.59
  299.1 1.9 collective-permute-start.34
  302.2 2.0 collective-permute-start.41
  304.8 1.9 collective-permute-start.19
  306.7 12.7 %collective-permute-done.34 = f32[32,2048]{1,0:T(8,128)S(1)} collective-permute-done((f32[32,2048]{1,0:T(8,128)S(1)}, f32[32,2048]{1,0:T(8,128)S(1)}, u32[]{:S(2)}, u32[]{:S(2)}) %collective-permute-start.34) | collective-permute-done | bytes 262176 | tf_op jit(solution)/shard_map/ppermute | solution.py:506
  322.8 2.1 collective-permute-start.60
  325.3 3.3 collective-permute-done.26
  330.9 5.4 %collective-permute-done.60 = f32[32,4224]{1,0:T(8,128)S(1)} collective-permute-done((f32[32,4224]{1,0:T(8,128)S(1)}, f32[32,4224]{1,0:T(8,128)S(1)}, u32[]{:S(2)}, u32[]{:S(2)}) %collective-permute-start.60) | collective-permute-done | bytes 540704 | tf_op jit(solution)/shard_map/ppermute | solution.py:507
  (244 shorter events, 64.7 us)
Async XLA Ops:
  0.7 56.3 %copy-start = (bf16[1024,1408]{1,0:T(8,128)(2,1)S(1)}, bf16[1024,1408]{1,0:T(8,128)(2,1)}, u32[]{:S(2)}) copy-start(bf16[1024,1408]{1,0:T(8,128)(2,1)} %param.42) | copy-start | bytes 8650756
  27.5 26.5 %collective-permute-start = (f32[256,1024]{1,0:T(8,128)}, f32[256,1024]{1,0:T(8,128)}, u32[]{:S(2)}, u32[]{:S(2)}) collective-permute-start(f32[256,1024]{1,0:T(8,128)} %fusion.91), channel_id=1, source_target_pairs={{0,1},{1,0},{2,3},{3,2},{4,5},{5,4},{6,7},{7,6},{8,9},{9,8},{10,11... | collective-permute-start | bytes 3145736 | tf_op jit(solution)/shard_map/ppermute | solution.py:442
  37.7 80.4 %collective-permute-start.43 = (f32[512,256]{1,0:T(8,128)}, f32[512,256]{1,0:T(8,128)}, u32[]{:S(2)}, u32[]{:S(2)}) collective-permute-start(f32[512,256]{1,0:T(8,128)} %fusion.50), channel_id=1, source_target_pairs={{0,2},{2,0},{4,6},{6,4},{8,10},{10,8},{12,14},{14,12},{16,18},{18,... | collective-permute-start | bytes 1572872 | tf_op jit(solution)/shard_map/ppermute | solution.py:442
  55.8 33.4 %copy-start.3 = (f32[256,1024]{1,0:T(8,128)}, f32[256,1024]{1,0:T(8,128)S(1)}, u32[]{:S(2)}) copy-start(f32[256,1024]{1,0:T(8,128)S(1)} %get-tuple-element.53) | copy-start | bytes 3145732
  62.6 26.1 %collective-permute-start.1 = (f32[256,1024]{1,0:T(8,128)S(1)}, f32[256,1024]{1,0:T(8,128)S(1)}, u32[]{:S(2)}, u32[]{:S(2)}) collective-permute-start(f32[256,1024]{1,0:T(8,128)S(1)} %convolution_add_fusion), channel_id=1, source_target_pairs={{0,1},{1,0},{2,3},{3,2},{4,5},{5,4},{6,7},{7,6},{8,9},{9,8},{10,11... | collective-permute-start | bytes 3145736 | tf_op jit(solution)/shard_map/ppermute | solution.py:442
  67.7 45.9 %collective-permute-start.2 = (f32[256,1024]{1,0:T(8,128)}, f32[256,1024]{1,0:T(8,128)}, u32[]{:S(2)}, u32[]{:S(2)}) collective-permute-start(f32[256,1024]{1,0:T(8,128)} %fusion.93), channel_id=1, source_target_pairs={{0,1},{1,0},{2,3},{3,2},{4,5},{5,4},{6,7},{7,6},{8,9},{9,8},{10,11... | collective-permute-start | bytes 3145736 | tf_op jit(solution)/shard_map/ppermute | solution.py:442
  68.0 52.0 %collective-permute-start.44 = (f32[256,1408]{1,0:T(8,128)}, f32[256,1408]{1,0:T(8,128)}, u32[]{:S(2)}, u32[]{:S(2)}) collective-permute-start(f32[256,1408]{1,0:T(8,128)} %get-tuple-element.128), channel_id=1, source_target_pairs={{0,2},{2,0},{4,6},{6,4},{8,10},{10,8},{12,14},{14,12},{16,18},{18,... | collective-permute-start | bytes 4325384 | tf_op jit(solution)/shard_map/ppermute | solution.py:442
  68.0 52.3 %collective-permute-start.45 = (f32[256,1408]{1,0:T(8,128)}, f32[256,1408]{1,0:T(8,128)}, u32[]{:S(2)}, u32[]{:S(2)}) collective-permute-start(f32[256,1408]{1,0:T(8,128)} %get-tuple-element.74), channel_id=1, source_target_pairs={{0,2},{2,0},{4,6},{6,4},{8,10},{10,8},{12,14},{14,12},{16,18},{18,... | collective-permute-start | bytes 4325384 | tf_op jit(solution)/shard_map/ppermute | solution.py:442
  88.7 31.5 %collective-permute-start.46 = (f32[256,1408]{1,0:T(8,128)}, f32[256,1408]{1,0:T(8,128)}, u32[]{:S(2)}, u32[]{:S(2)}) collective-permute-start(f32[256,1408]{1,0:T(8,128)} %get-tuple-element.130), channel_id=1, source_target_pairs={{0,2},{2,0},{4,6},{6,4},{8,10},{10,8},{12,14},{14,12},{16,18},{18,... | collective-permute-start | bytes 4325384 | tf_op jit(solution)/shard_map/ppermute | solution.py:442
  113.6 4.6 %collective-permute-start.42 = (f32[512,256]{1,0:T(8,128)}, f32[512,256]{1,0:T(8,128)}, u32[]{:S(2)}, u32[]{:S(2)}) collective-permute-start(f32[512,256]{1,0:T(8,128)} %fusion), channel_id=1, source_target_pairs={{0,2},{2,0},{4,6},{6,4},{8,10},{10,8},{12,14},{14,12},{16,18},{18,... | collective-permute-start | bytes 1572872 | tf_op jit(solution)/shard_map/ppermute | solution.py:442
  118.2 74.0 %collective-permute-start.9 = (f32[512,256]{1,0:T(8,128)}, f32[512,256]{1,0:T(8,128)S(1)}, u32[]{:S(2)}, u32[]{:S(2)}) collective-permute-start(f32[512,256]{1,0:T(8,128)} %fusion.53), channel_id=1, source_target_pairs={{0,2},{2,0},{4,6},{6,4},{8,10},{10,8},{12,14},{14,12},{16,18},{18,... | collective-permute-start | bytes 1572872 | tf_op jit(solution)/shard_map/ppermute | solution.py:442
  118.2 25.9 %collective-permute-start.3 = (f32[256,1024]{1,0:T(8,128)}, f32[256,1024]{1,0:T(8,128)}, u32[]{:S(2)}, u32[]{:S(2)}) collective-permute-start(f32[256,1024]{1,0:T(8,128)} %get-tuple-element.55), channel_id=1, source_target_pairs={{0,1},{1,0},{2,3},{3,2},{4,5},{5,4},{6,7},{7,6},{8,9},{9,8},{10,11... | collective-permute-start | bytes 3145736 | tf_op jit(solution)/shard_map/ppermute | solution.py:442
  120.0 24.1 %collective-permute-start.4 = (f32[1,256]{1,0:T(1,128)S(1)}, f32[1,256]{1,0:T(1,128)S(1)}, u32[]{:S(2)}, u32[]{:S(2)}) collective-permute-start(f32[1,256]{1,0:T(1,128)S(1)} %copy-done.35), channel_id=1, source_target_pairs={{0,1},{1,0},{2,3},{3,2},{4,5},{5,4},{6,7},{7,6},{8,9},{9,8},{10,11... | collective-permute-start | bytes 3080 | tf_op jit(solution)/shard_map/ppermute | solution.py:442
  131.6 17.2 %collective-permute-start.54 = (f32[32,4224]{1,0:T(8,128)}, f32[32,4224]{1,0:T(8,128)}, u32[]{:S(2)}, u32[]{:S(2)}) collective-permute-start(f32[32,4224]{1,0:T(8,128)} %get-tuple-element.94), channel_id=1, source_target_pairs={{8,0},{10,2},{16,8},{18,10},{24,16},{26,18},{28,24},{30,26},{20,28... | collective-permute-start | bytes 1622024 | tf_op jit(solution)/shard_map/ppermute | solution.py:507
  133.3 17.3 %collective-permute-start.47 = (f32[32,4224]{1,0:T(8,128)}, f32[32,4224]{1,0:T(8,128)}, u32[]{:S(2)}, u32[]{:S(2)}) collective-permute-start(f32[32,4224]{1,0:T(8,128)} %get-tuple-element.95), channel_id=1, source_target_pairs={{0,8},{2,10},{8,16},{10,18},{16,24},{18,26},{24,28},{26,30},{28,20... | collective-permute-start | bytes 1622024 | tf_op jit(solution)/shard_map/ppermute | solution.py:506
  144.1 48.1 %collective-permute-start.12 = (f32[256,1024]{1,0:T(8,128)}, f32[256,1024]{1,0:T(8,128)S(1)}, u32[]{:S(2)}, u32[]{:S(2)}) collective-permute-start(f32[256,1024]{1,0:T(8,128)} %get-tuple-element.66), channel_id=1, source_target_pairs={{0,2},{2,0},{4,6},{6,4},{8,10},{10,8},{12,14},{14,12},{16,18},{18,... | collective-permute-start | bytes 3145736 | tf_op jit(solution)/shard_map/ppermute | solution.py:442
  146.9 1.8 collective-permute-start.5
  148.7 45.5 %collective-permute-start.27 = (f32[256,1536]{1,0:T(8,128)}, f32[256,1536]{1,0:T(8,128)}, u32[]{:S(2)}, u32[]{:S(2)}) collective-permute-start(f32[256,1536]{1,0:T(8,128)} %get-tuple-element.67.refs_4_), channel_id=1, source_target_pairs={{0,2},{2,0},{4,6},{6,4},{8,10},{10,8},{12,14},{14,12},{16,18},{18,... | collective-permute-start | bytes 4718600 | tf_op jit(solution)/shard_map/ppermute | solution.py:442
  148.8 4.9 %collective-permute-start.6 = (f32[154,128]{1,0:T(8,128)S(1)}, f32[154,128]{1,0:T(8,128)S(1)}, u32[]{:S(2)}, u32[]{:S(2)}) collective-permute-start(f32[154,128]{1,0:T(8,128)S(1)} %add.291), channel_id=1, source_target_pairs={{0,4},{2,6},{4,0},{6,2},{8,12},{10,14},{12,8},{14,10},{16,20},{18,... | collective-permute-start | bytes 236552 | tf_op jit(solution)/shard_map/ppermute | solution.py:451
  153.2 25.7 %collective-permute-start.55 = (f32[32,4224]{1,0:T(8,128)}, f32[32,4224]{1,0:T(8,128)}, u32[]{:S(2)}, u32[]{:S(2)}) collective-permute-start(f32[32,4224]{1,0:T(8,128)} %get-tuple-element.92), channel_id=1, source_target_pairs={{8,0},{10,2},{16,8},{18,10},{24,16},{26,18},{28,24},{30,26},{20,28... | collective-permute-start | bytes 1622024 | tf_op jit(solution)/shard_map/ppermute | solution.py:507
  153.7 15.8 %collective-permute-start.7 = (f32[154,128]{1,0:T(8,128)S(1)}, f32[154,128]{1,0:T(8,128)S(1)}, u32[]{:S(2)}, u32[]{:S(2)}) collective-permute-start(f32[154,128]{1,0:T(8,128)S(1)} %add.292), channel_id=1, source_target_pairs={{0,8},{2,10},{4,12},{6,14},{8,0},{10,2},{12,4},{14,6},{16,24},{18,... | collective-permute-start | bytes 236552 | tf_op jit(solution)/shard_map/ppermute | solution.py:451
  169.5 5.7 %collective-permute-start.8 = (f32[154,128]{1,0:T(8,128)S(1)}, f32[154,128]{1,0:T(8,128)S(1)}, u32[]{:S(2)}, u32[]{:S(2)}) collective-permute-start(f32[154,128]{1,0:T(8,128)S(1)} %add.293), channel_id=1, source_target_pairs={{0,16},{2,18},{4,20},{6,22},{8,24},{10,26},{12,28},{14,30},{16,0},... | collective-permute-start | bytes 236552 | tf_op jit(solution)/shard_map/ppermute | solution.py:451
  175.2 13.6 %collective-permute-start.48 = (f32[32,4224]{1,0:T(8,128)}, f32[32,4224]{1,0:T(8,128)S(1)}, u32[]{:S(2)}, u32[]{:S(2)}) collective-permute-start(f32[32,4224]{1,0:T(8,128)} %get-tuple-element.93), channel_id=1, source_target_pairs={{0,8},{2,10},{8,16},{10,18},{16,24},{18,26},{24,28},{26,30},{28,20... | collective-permute-start | bytes 1622024 | tf_op jit(solution)/shard_map/ppermute | solution.py:506
  178.9 15.3 %collective-permute-start.10 = (f32[512,256]{1,0:T(8,128)}, f32[512,256]{1,0:T(8,128)S(1)}, u32[]{:S(2)}, u32[]{:S(2)}) collective-permute-start(f32[512,256]{1,0:T(8,128)} %fusion.1), channel_id=1, source_target_pairs={{0,2},{2,0},{4,6},{6,4},{8,10},{10,8},{12,14},{14,12},{16,18},{18,... | collective-permute-start | bytes 1572872 | tf_op jit(solution)/shard_map/ppermute | solution.py:442
  189.7 15.0 %collective-permute-start.11 = (f32[256,1536]{1,0:T(8,128)}, f32[256,1536]{1,0:T(8,128)}, u32[]{:S(2)}, u32[]{:S(2)}) collective-permute-start(f32[256,1536]{1,0:T(8,128)} %get-tuple-element.65.refs_4_), channel_id=1, source_target_pairs={{0,2},{2,0},{4,6},{6,4},{8,10},{10,8},{12,14},{14,12},{16,18},{18,... | collective-permute-start | bytes 4718600 | tf_op jit(solution)/shard_map/ppermute | solution.py:442
  192.1 32.8 %collective-permute-start.56 = (f32[32,4224]{1,0:T(8,128)}, f32[32,4224]{1,0:T(8,128)}, u32[]{:S(2)}, u32[]{:S(2)}) collective-permute-start(f32[32,4224]{1,0:T(8,128)} %get-tuple-element.90), channel_id=1, source_target_pairs={{8,0},{10,2},{16,8},{18,10},{24,16},{26,18},{28,24},{30,26},{20,28... | collective-permute-start | bytes 1622024 | tf_op jit(solution)/shard_map/ppermute | solution.py:507
  192.2 32.9 %collective-permute-start.49 = (f32[32,4224]{1,0:T(8,128)S(1)}, f32[32,4224]{1,0:T(8,128)}, u32[]{:S(2)}, u32[]{:S(2)}) collective-permute-start(f32[32,4224]{1,0:T(8,128)S(1)} %get-tuple-element.91), channel_id=1, source_target_pairs={{0,8},{2,10},{8,16},{10,18},{16,24},{18,26},{24,28},{26,30},{28,20... | collective-permute-start | bytes 1622024 | tf_op jit(solution)/shard_map/ppermute | solution.py:506
  202.6 10.4 %collective-permute-start.28 = (f32[32,2048]{1,0:T(8,128)S(1)}, f32[32,2048]{1,0:T(8,128)S(1)}, u32[]{:S(2)}, u32[]{:S(2)}) collective-permute-start(f32[32,2048]{1,0:T(8,128)S(1)} %get-tuple-element.126), channel_id=1, source_target_pairs={{0,8},{2,10},{8,16},{10,18},{16,24},{18,26},{24,28},{26,30},{28,20... | collective-permute-start | bytes 786440 | tf_op jit(solution)/shard_map/ppermute | solution.py:506
  203.0 11.6 %collective-permute-start.35 = (f32[32,2048]{1,0:T(8,128)S(1)}, f32[32,2048]{1,0:T(8,128)S(1)}, u32[]{:S(2)}, u32[]{:S(2)}) collective-permute-start(f32[32,2048]{1,0:T(8,128)S(1)} %get-tuple-element.127), channel_id=1, source_target_pairs={{8,0},{10,2},{16,8},{18,10},{24,16},{26,18},{28,24},{30,26},{20,28... | collective-permute-start | bytes 786440 | tf_op jit(solution)/shard_map/ppermute | solution.py:507
  211.3 19.6 %copy-start.6 = (f32[512,2048]{1,0:T(8,128)S(1)}, f32[512,2048]{1,0:T(8,128)}, u32[]{:S(2)}) copy-start(f32[512,2048]{1,0:T(8,128)} %shard_map.386) | copy-start | bytes 12582916
  212.5 9.2 %collective-permute-start.13 = (f32[32,2048]{1,0:T(8,128)S(1)}, f32[32,2048]{1,0:T(8,128)S(1)}, u32[]{:S(2)}, u32[]{:S(2)}) collective-permute-start(f32[32,2048]{1,0:T(8,128)S(1)} %get-tuple-element.110), channel_id=1, source_target_pairs={{0,8},{2,10},{8,16},{10,18},{16,24},{18,26},{24,28},{26,30},{28,20... | collective-permute-start | bytes 786440 | tf_op jit(solution)/shard_map/ppermute | solution.py:506
  213.0 8.9 %collective-permute-start.20 = (f32[32,2048]{1,0:T(8,128)S(1)}, f32[32,2048]{1,0:T(8,128)S(1)}, u32[]{:S(2)}, u32[]{:S(2)}) collective-permute-start(f32[32,2048]{1,0:T(8,128)S(1)} %get-tuple-element.111), channel_id=1, source_target_pairs={{8,0},{10,2},{16,8},{18,10},{24,16},{26,18},{28,24},{30,26},{20,28... | collective-permute-start | bytes 786440 | tf_op jit(solution)/shard_map/ppermute | solution.py:507
  215.7 12.8 %collective-permute-start.29 = (f32[32,2048]{1,0:T(8,128)S(1)}, f32[32,2048]{1,0:T(8,128)S(1)}, u32[]{:S(2)}, u32[]{:S(2)}) collective-permute-start(f32[32,2048]{1,0:T(8,128)S(1)} %get-tuple-element.124), channel_id=1, source_target_pairs={{0,8},{2,10},{8,16},{10,18},{16,24},{18,26},{24,28},{26,30},{28,20... | collective-permute-start | bytes 786440 | tf_op jit(solution)/shard_map/ppermute | solution.py:506
  221.7 9.2 %collective-permute-start.36 = (f32[32,2048]{1,0:T(8,128)S(1)}, f32[32,2048]{1,0:T(8,128)S(1)}, u32[]{:S(2)}, u32[]{:S(2)}) collective-permute-start(f32[32,2048]{1,0:T(8,128)S(1)} %get-tuple-element.125), channel_id=1, source_target_pairs={{8,0},{10,2},{16,8},{18,10},{24,16},{26,18},{28,24},{30,26},{20,28... | collective-permute-start | bytes 786440 | tf_op jit(solution)/shard_map/ppermute | solution.py:507
  223.0 10.0 %collective-permute-start.14 = (f32[32,2048]{1,0:T(8,128)S(1)}, f32[32,2048]{1,0:T(8,128)S(1)}, u32[]{:S(2)}, u32[]{:S(2)}) collective-permute-start(f32[32,2048]{1,0:T(8,128)S(1)} %get-tuple-element.108), channel_id=1, source_target_pairs={{0,8},{2,10},{8,16},{10,18},{16,24},{18,26},{24,28},{26,30},{28,20... | collective-permute-start | bytes 786440 | tf_op jit(solution)/shard_map/ppermute | solution.py:506
  224.9 11.6 %collective-permute-start.21 = (f32[32,2048]{1,0:T(8,128)S(1)}, f32[32,2048]{1,0:T(8,128)S(1)}, u32[]{:S(2)}, u32[]{:S(2)}) collective-permute-start(f32[32,2048]{1,0:T(8,128)S(1)} %get-tuple-element.109), channel_id=1, source_target_pairs={{8,0},{10,2},{16,8},{18,10},{24,16},{26,18},{28,24},{30,26},{20,28... | collective-permute-start | bytes 786440 | tf_op jit(solution)/shard_map/ppermute | solution.py:507
  226.8 33.1 %collective-permute-start.57 = (f32[32,4224]{1,0:T(8,128)S(1)}, f32[32,4224]{1,0:T(8,128)S(1)}, u32[]{:S(2)}, u32[]{:S(2)}) collective-permute-start(f32[32,4224]{1,0:T(8,128)S(1)} %get-tuple-element.88), channel_id=1, source_target_pairs={{8,0},{10,2},{16,8},{18,10},{24,16},{26,18},{28,24},{30,26},{20,28... | collective-permute-start | bytes 1622024 | tf_op jit(solution)/shard_map/ppermute | solution.py:507
  228.5 31.5 %collective-permute-start.50 = (f32[32,4224]{1,0:T(8,128)S(1)}, f32[32,4224]{1,0:T(8,128)S(1)}, u32[]{:S(2)}, u32[]{:S(2)}) collective-permute-start(f32[32,4224]{1,0:T(8,128)S(1)} %get-tuple-element.89), channel_id=1, source_target_pairs={{0,8},{2,10},{8,16},{10,18},{16,24},{18,26},{24,28},{26,30},{28,20... | collective-permute-start | bytes 1622024 | tf_op jit(solution)/shard_map/ppermute | solution.py:506
  231.0 19.2 %collective-permute-start.30 = (f32[32,2048]{1,0:T(8,128)S(1)}, f32[32,2048]{1,0:T(8,128)S(1)}, u32[]{:S(2)}, u32[]{:S(2)}) collective-permute-start(f32[32,2048]{1,0:T(8,128)S(1)} %get-tuple-element.122), channel_id=1, source_target_pairs={{0,8},{2,10},{8,16},{10,18},{16,24},{18,26},{24,28},{26,30},{28,20... | collective-permute-start | bytes 786440 | tf_op jit(solution)/shard_map/ppermute | solution.py:506
  233.0 18.1 %collective-permute-start.37 = (f32[32,2048]{1,0:T(8,128)S(1)}, f32[32,2048]{1,0:T(8,128)S(1)}, u32[]{:S(2)}, u32[]{:S(2)}) collective-permute-start(f32[32,2048]{1,0:T(8,128)S(1)} %get-tuple-element.123), channel_id=1, source_target_pairs={{8,0},{10,2},{16,8},{18,10},{24,16},{26,18},{28,24},{30,26},{20,28... | collective-permute-start | bytes 786440 | tf_op jit(solution)/shard_map/ppermute | solution.py:507
  236.6 19.2 %collective-permute-start.15 = (f32[32,2048]{1,0:T(8,128)S(1)}, f32[32,2048]{1,0:T(8,128)S(1)}, u32[]{:S(2)}, u32[]{:S(2)}) collective-permute-start(f32[32,2048]{1,0:T(8,128)S(1)} %get-tuple-element.106), channel_id=1, source_target_pairs={{0,8},{2,10},{8,16},{10,18},{16,24},{18,26},{24,28},{26,30},{28,20... | collective-permute-start | bytes 786440 | tf_op jit(solution)/shard_map/ppermute | solution.py:506
  250.2 7.6 %collective-permute-start.22 = (f32[32,2048]{1,0:T(8,128)S(1)}, f32[32,2048]{1,0:T(8,128)S(1)}, u32[]{:S(2)}, u32[]{:S(2)}) collective-permute-start(f32[32,2048]{1,0:T(8,128)S(1)} %get-tuple-element.107), channel_id=1, source_target_pairs={{8,0},{10,2},{16,8},{18,10},{24,16},{26,18},{28,24},{30,26},{20,28... | collective-permute-start | bytes 786440 | tf_op jit(solution)/shard_map/ppermute | solution.py:507
  251.2 11.8 %collective-permute-start.31 = (f32[32,2048]{1,0:T(8,128)S(1)}, f32[32,2048]{1,0:T(8,128)S(1)}, u32[]{:S(2)}, u32[]{:S(2)}) collective-permute-start(f32[32,2048]{1,0:T(8,128)S(1)} %get-tuple-element.120), channel_id=1, source_target_pairs={{0,8},{2,10},{8,16},{10,18},{16,24},{18,26},{24,28},{26,30},{28,20... | collective-permute-start | bytes 786440 | tf_op jit(solution)/shard_map/ppermute | solution.py:506
  255.8 9.2 %collective-permute-start.38 = (f32[32,2048]{1,0:T(8,128)S(1)}, f32[32,2048]{1,0:T(8,128)S(1)}, u32[]{:S(2)}, u32[]{:S(2)}) collective-permute-start(f32[32,2048]{1,0:T(8,128)S(1)} %get-tuple-element.121), channel_id=1, source_target_pairs={{8,0},{10,2},{16,8},{18,10},{24,16},{26,18},{28,24},{30,26},{20,28... | collective-permute-start | bytes 786440 | tf_op jit(solution)/shard_map/ppermute | solution.py:507
  257.8 9.2 %collective-permute-start.16 = (f32[32,2048]{1,0:T(8,128)S(1)}, f32[32,2048]{1,0:T(8,128)S(1)}, u32[]{:S(2)}, u32[]{:S(2)}) collective-permute-start(f32[32,2048]{1,0:T(8,128)S(1)} %get-tuple-element.104), channel_id=1, source_target_pairs={{0,8},{2,10},{8,16},{10,18},{16,24},{18,26},{24,28},{26,30},{28,20... | collective-permute-start | bytes 786440 | tf_op jit(solution)/shard_map/ppermute | solution.py:506
  259.9 10.7 %collective-permute-start.23 = (f32[32,2048]{1,0:T(8,128)S(1)}, f32[32,2048]{1,0:T(8,128)S(1)}, u32[]{:S(2)}, u32[]{:S(2)}) collective-permute-start(f32[32,2048]{1,0:T(8,128)S(1)} %get-tuple-element.105), channel_id=1, source_target_pairs={{8,0},{10,2},{16,8},{18,10},{24,16},{26,18},{28,24},{30,26},{20,28... | collective-permute-start | bytes 786440 | tf_op jit(solution)/shard_map/ppermute | solution.py:507
  261.3 34.2 %collective-permute-start.58 = (f32[32,4224]{1,0:T(8,128)S(1)}, f32[32,4224]{1,0:T(8,128)S(1)}, u32[]{:S(2)}, u32[]{:S(2)}) collective-permute-start(f32[32,4224]{1,0:T(8,128)S(1)} %get-tuple-element.86), channel_id=1, source_target_pairs={{8,0},{10,2},{16,8},{18,10},{24,16},{26,18},{28,24},{30,26},{20,28... | collective-permute-start | bytes 1622024 | tf_op jit(solution)/shard_map/ppermute | solution.py:507
  263.0 32.4 %collective-permute-start.51 = (f32[32,4224]{1,0:T(8,128)S(1)}, f32[32,4224]{1,0:T(8,128)S(1)}, u32[]{:S(2)}, u32[]{:S(2)}) collective-permute-start(f32[32,4224]{1,0:T(8,128)S(1)} %get-tuple-element.87), channel_id=1, source_target_pairs={{0,8},{2,10},{8,16},{10,18},{16,24},{18,26},{24,28},{26,30},{28,20... | collective-permute-start | bytes 1622024 | tf_op jit(solution)/shard_map/ppermute | solution.py:506
  265.1 19.2 %collective-permute-start.32 = (f32[32,2048]{1,0:T(8,128)S(1)}, f32[32,2048]{1,0:T(8,128)S(1)}, u32[]{:S(2)}, u32[]{:S(2)}) collective-permute-start(f32[32,2048]{1,0:T(8,128)S(1)} %get-tuple-element.118), channel_id=1, source_target_pairs={{0,8},{2,10},{8,16},{10,18},{16,24},{18,26},{24,28},{26,30},{28,20... | collective-permute-start | bytes 786440 | tf_op jit(solution)/shard_map/ppermute | solution.py:506
  267.1 19.2 %collective-permute-start.39 = (f32[32,2048]{1,0:T(8,128)S(1)}, f32[32,2048]{1,0:T(8,128)S(1)}, u32[]{:S(2)}, u32[]{:S(2)}) collective-permute-start(f32[32,2048]{1,0:T(8,128)S(1)} %get-tuple-element.119), channel_id=1, source_target_pairs={{8,0},{10,2},{16,8},{18,10},{24,16},{26,18},{28,24},{30,26},{20,28... | collective-permute-start | bytes 786440 | tf_op jit(solution)/shard_map/ppermute | solution.py:507
  270.7 19.2 %collective-permute-start.17 = (f32[32,2048]{1,0:T(8,128)S(1)}, f32[32,2048]{1,0:T(8,128)S(1)}, u32[]{:S(2)}, u32[]{:S(2)}) collective-permute-start(f32[32,2048]{1,0:T(8,128)S(1)} %get-tuple-element.102), channel_id=1, source_target_pairs={{0,8},{2,10},{8,16},{10,18},{16,24},{18,26},{24,28},{26,30},{28,20... | collective-permute-start | bytes 786440 | tf_op jit(solution)/shard_map/ppermute | solution.py:506
  284.3 8.1 %collective-permute-start.24 = (f32[32,2048]{1,0:T(8,128)S(1)}, f32[32,2048]{1,0:T(8,128)S(1)}, u32[]{:S(2)}, u32[]{:S(2)}) collective-permute-start(f32[32,2048]{1,0:T(8,128)S(1)} %get-tuple-element.103), channel_id=1, source_target_pairs={{8,0},{10,2},{16,8},{18,10},{24,16},{26,18},{28,24},{30,26},{20,28... | collective-permute-start | bytes 786440 | tf_op jit(solution)/shard_map/ppermute | solution.py:507
  286.3 12.1 %collective-permute-start.33 = (f32[32,2048]{1,0:T(8,128)S(1)}, f32[32,2048]{1,0:T(8,128)S(1)}, u32[]{:S(2)}, u32[]{:S(2)}) collective-permute-start(f32[32,2048]{1,0:T(8,128)S(1)} %get-tuple-element.116), channel_id=1, source_target_pairs={{0,8},{2,10},{8,16},{10,18},{16,24},{18,26},{24,28},{26,30},{28,20... | collective-permute-start | bytes 786440 | tf_op jit(solution)/shard_map/ppermute | solution.py:506
  289.9 9.2 %collective-permute-start.40 = (f32[32,2048]{1,0:T(8,128)S(1)}, f32[32,2048]{1,0:T(8,128)S(1)}, u32[]{:S(2)}, u32[]{:S(2)}) collective-permute-start(f32[32,2048]{1,0:T(8,128)S(1)} %get-tuple-element.117), channel_id=1, source_target_pairs={{8,0},{10,2},{16,8},{18,10},{24,16},{26,18},{28,24},{30,26},{20,28... | collective-permute-start | bytes 786440 | tf_op jit(solution)/shard_map/ppermute | solution.py:507
  292.5 9.7 %collective-permute-start.18 = (f32[32,2048]{1,0:T(8,128)S(1)}, f32[32,2048]{1,0:T(8,128)S(1)}, u32[]{:S(2)}, u32[]{:S(2)}) collective-permute-start(f32[32,2048]{1,0:T(8,128)S(1)} %get-tuple-element.100), channel_id=1, source_target_pairs={{0,8},{2,10},{8,16},{10,18},{16,24},{18,26},{24,28},{26,30},{28,20... | collective-permute-start | bytes 786440 | tf_op jit(solution)/shard_map/ppermute | solution.py:506
  295.5 9.2 %collective-permute-start.25 = (f32[32,2048]{1,0:T(8,128)S(1)}, f32[32,2048]{1,0:T(8,128)S(1)}, u32[]{:S(2)}, u32[]{:S(2)}) collective-permute-start(f32[32,2048]{1,0:T(8,128)S(1)} %get-tuple-element.101), channel_id=1, source_target_pairs={{8,0},{10,2},{16,8},{18,10},{24,16},{26,18},{28,24},{30,26},{20,28... | collective-permute-start | bytes 786440 | tf_op jit(solution)/shard_map/ppermute | solution.py:507
  296.8 24.7 %collective-permute-start.59 = (f32[32,4224]{1,0:T(8,128)S(1)}, f32[32,4224]{1,0:T(8,128)S(1)}, u32[]{:S(2)}, u32[]{:S(2)}) collective-permute-start(f32[32,4224]{1,0:T(8,128)S(1)} %get-tuple-element.84), channel_id=1, source_target_pairs={{8,0},{10,2},{16,8},{18,10},{24,16},{26,18},{28,24},{30,26},{20,28... | collective-permute-start | bytes 1622024 | tf_op jit(solution)/shard_map/ppermute | solution.py:507
  298.4 23.1 %collective-permute-start.52 = (f32[32,4224]{1,0:T(8,128)S(1)}, f32[32,4224]{1,0:T(8,128)S(1)}, u32[]{:S(2)}, u32[]{:S(2)}) collective-permute-start(f32[32,4224]{1,0:T(8,128)S(1)} %get-tuple-element.85), channel_id=1, source_target_pairs={{0,8},{2,10},{8,16},{10,18},{16,24},{18,26},{24,28},{26,30},{28,20... | collective-permute-start | bytes 1622024 | tf_op jit(solution)/shard_map/ppermute | solution.py:506
  299.1 20.2 %collective-permute-start.34 = (f32[32,2048]{1,0:T(8,128)S(1)}, f32[32,2048]{1,0:T(8,128)S(1)}, u32[]{:S(2)}, u32[]{:S(2)}) collective-permute-start(f32[32,2048]{1,0:T(8,128)S(1)} %get-tuple-element.114), channel_id=1, source_target_pairs={{0,8},{2,10},{8,16},{10,18},{16,24},{18,26},{24,28},{26,30},{28,20... | collective-permute-start | bytes 786440 | tf_op jit(solution)/shard_map/ppermute | solution.py:506
  302.2 19.2 %collective-permute-start.41 = (f32[32,2048]{1,0:T(8,128)S(1)}, f32[32,2048]{1,0:T(8,128)S(1)}, u32[]{:S(2)}, u32[]{:S(2)}) collective-permute-start(f32[32,2048]{1,0:T(8,128)S(1)} %get-tuple-element.115), channel_id=1, source_target_pairs={{8,0},{10,2},{16,8},{18,10},{24,16},{26,18},{28,24},{30,26},{20,28... | collective-permute-start | bytes 786440 | tf_op jit(solution)/shard_map/ppermute | solution.py:507
  304.8 20.5 %collective-permute-start.19 = (f32[32,2048]{1,0:T(8,128)S(1)}, f32[32,2048]{1,0:T(8,128)S(1)}, u32[]{:S(2)}, u32[]{:S(2)}) collective-permute-start(f32[32,2048]{1,0:T(8,128)S(1)} %get-tuple-element.98), channel_id=1, source_target_pairs={{0,8},{2,10},{8,16},{10,18},{16,24},{18,26},{24,28},{26,30},{28,20... | collective-permute-start | bytes 786440 | tf_op jit(solution)/shard_map/ppermute | solution.py:506
  319.4 9.2 %collective-permute-start.26 = (f32[32,2048]{1,0:T(8,128)S(1)}, f32[32,2048]{1,0:T(8,128)S(1)}, u32[]{:S(2)}, u32[]{:S(2)}) collective-permute-start(f32[32,2048]{1,0:T(8,128)S(1)} %get-tuple-element.99), channel_id=1, source_target_pairs={{8,0},{10,2},{16,8},{18,10},{24,16},{26,18},{28,24},{30,26},{20,28... | collective-permute-start | bytes 786440 | tf_op jit(solution)/shard_map/ppermute | solution.py:507
  322.8 13.5 %collective-permute-start.60 = (f32[32,4224]{1,0:T(8,128)S(1)}, f32[32,4224]{1,0:T(8,128)S(1)}, u32[]{:S(2)}, u32[]{:S(2)}) collective-permute-start(f32[32,4224]{1,0:T(8,128)S(1)} %get-tuple-element.82), channel_id=1, source_target_pairs={{8,0},{10,2},{16,8},{18,10},{24,16},{26,18},{28,24},{30,26},{20,28... | collective-permute-start | bytes 1622024 | tf_op jit(solution)/shard_map/ppermute | solution.py:507
  324.9 11.4 %collective-permute-start.53 = (f32[32,4224]{1,0:T(8,128)S(1)}, f32[32,4224]{1,0:T(8,128)S(1)}, u32[]{:S(2)}, u32[]{:S(2)}) collective-permute-start(f32[32,4224]{1,0:T(8,128)S(1)} %get-tuple-element.83), channel_id=1, source_target_pairs={{0,8},{2,10},{8,16},{10,18},{16,24},{18,26},{24,28},{26,30},{28,20... | collective-permute-start | bytes 1622024 | tf_op jit(solution)/shard_map/ppermute | solution.py:506
  (36 other events, 171.7 us)
where the time goes:
time: 339 us
  waiting for transfers between devices  134 us (40%)
  starting transfers between devices  61.1 us (18%)
  Pallas kernels  56.7 us (17%)
  matrix products  37.1 us (11%)
  other arithmetic  33.6 us (10%)
  local copies, waits for them, and re-layouts  13.2 us (4%)
    ppermute x21, waiting for transfers between devices, reduce(): going = lax.ppermute(going, self.axis, self.up)  62.1 us
    ppermute x15, waiting for transfers between devices, swap(): return lax.ppermute(value, axis, [(i, i ^ 1) for i in range(size)])  37 us
    ppermute x21, starting transfers between devices, reduce(): coming = lax.ppermute(coming, self.axis, self.down)  22.9 us
    ppermute x21, starting transfers between devices, reduce(): going = lax.ppermute(going, self.axis, self.up)  22.9 us
    pallas_call x3, Pallas kernels, weight_grads(): pl.pallas_call(functools.partial(grads_kernel, tuple((pair for pair, *_ i...  22 us
    ppermute x21, waiting for transfers between devices, reduce(): coming = lax.ppermute(coming, self.axis, self.down)  21 us
    pallas_call x2, Pallas kernels, mixer_backward(): pl.pallas_call(functools.partial(backward_kernel, first, heads, bool(befo...  20.9 us
    dot_general x12, matrix products, matmul_nt(): lax.dot_general(first_arr, second_arr, (((1,), (1,)), ((), ())), preferre...  18.7 us
  transfers between devices with their start and end apart: 61, of which 27 were waited for; matrix products, arithmetic and copies ran while one was open for 19% of the time, Pallas kernels for 13%

commit v1 on v0

--- a/solution.py
+++ b/solution.py
@@ -205,7 +205,7 @@
         new_ref[:, vs] = t.beta * t.v
         return carry
 
-    lax.fori_loop(0, heads, begin, 0)
+    lax.fori_loop(0, heads, begin, 0, unroll=2)
 
     def block_of(index):
         at = slice(index % blocks * chunk, (index % blocks + 1) * chunk)
@@ -480,13 +480,12 @@
         chips = jnp.asarray(order, jnp.int32)[(pos - 1 - turn) % self.count]
         start = chips[:, None, None] * (2 * self.block) + off
         shape = (self.count * self.block, width)
-        self.mine = (col == start + core * self.block).astype(bf16).reshape(shape)
-        self.other = (col == start + (1 - core) * self.block).astype(bf16).reshape(shape)
+        picks = [(col == start + side * self.block).reshape(shape) for side in (core, 1 - core)]
+        self.pick = jnp.concatenate(picks, axis=0).astype(bf16)
 
     def rows(self, source):
-        own = matmul_nt(self.mine, source).astype(bf16)
-        sent = swap(matmul_nt(self.other, source), self.axis)
-        return own, sent
+        both = matmul_nt(self.pick, source)
+        return both, swap(both[both.shape[0] // 2 :], self.axis)
 
     def reduce(self, partials):
         n, half = self.count, self.block // 2
@@ -521,7 +520,7 @@
     @pl.when(step == 0)
     def _():
         for pair in range(pairs):
-            rows_ref[pair, :, :depth] = row_refs[2 * pair][...]
+            rows_ref[pair, :, :depth] = row_refs[2 * pair][...].astype(bf16)
             rows_ref[pair, :, depth:] = row_refs[2 * pair + 1][...].astype(bf16)
 
     chosen = 0
@@ -633,7 +632,7 @@
     rows_two = ring.rows(h_two)
     ffn_cols = (d_pre_one, d_pre_three, hidden)
     ffn_sent = [swap(arr.astype(f32), DP) for arr in ffn_cols]
-    tall = rows_two[0].shape[0]
+    tall = rows_two[1].shape[0]
     ffn_grads = [(pair, own, sent, 0, own.shape[1]) for pair, own, sent in zip((0, 0, 1), ffn_cols, ffn_sent)]
     ffn_partial = weight_grads((rows_two, rows_out), ffn_grads, tall)
     ffn_sum = ring.reduce([ffn_partial])

time: 339 us -> 361 us (1.065)
  waiting for transfers between devices: 134 us -> 155 us
  matrix products: 37.1 us -> 32.5 us
  local copies, waits for them, and re-layouts: 13.2 us -> 17.3 us
    ppermute x15, waiting for transfers between devices: 37 us -> 56.3 us  [swap(): return lax.ppermute(value, axis, [(i, i ^ 1) for i in range(size)])]
    dot_general x12 -> x8, matrix products: 18.7 us -> 12.7 us  [matmul_nt(): lax.dot_general(first_arr, second_arr, (((1,), (1,)), ((), ())), preferre...]
  transfers between devices with their start and end apart: 61 -> 61, of which waited for: 27 -> 29; matrix products, arithmetic and copies ran while one was open for 19% -> 16% of each run, Pallas kernels for 13% -> 12%
where the time goes in v1:
time: 361 us; the launch traced here: 360 us
  waiting for transfers between devices  155 us (43%)
  starting transfers between devices  59.2 us (16%)
  Pallas kernels  57.1 us (16%)
  other arithmetic  35.5 us (10%)
  matrix products  32.5 us (9%)
  local copies, waits for them, and re-layouts  17.3 us (5%)
    ppermute x21, waiting for transfers between devices, reduce(): going = lax.ppermute(going, self.axis, self.up)  63 us
    ppermute x15, waiting for transfers between devices, swap(): return lax.ppermute(value, axis, [(i, i ^ 1) for i in range(size)])  56.3 us
    ppermute x21, starting transfers between devices, reduce(): coming = lax.ppermute(coming, self.axis, self.down)  23.2 us
    pallas_call x3, Pallas kernels, weight_grads(): pl.pallas_call(functools.partial(grads_kernel, tuple((pair for pair, *_ i...  22.4 us
    ppermute x21, waiting for transfers between devices, reduce(): coming = lax.ppermute(coming, self.axis, self.down)  21.9 us
    ppermute x21, starting transfers between devices, reduce(): going = lax.ppermute(going, self.axis, self.up)  21.3 us
    pallas_call x2, Pallas kernels, mixer_backward(): pl.pallas_call(functools.partial(backward_kernel, first, heads, bool(befo...  21 us
    ppermute x4, waiting for transfers between devices, sum_over(): other = lax.ppermute(value, axis, [(i, i ^ step) for i in range(size)])  14.3 us
  transfers between devices with their start and end apart: 61, of which 29 were waited for; matrix products, arithmetic and copies ran while one was open for 16% of the time, Pallas kernels for 12%

profile of v1, /device:TPU:0, one launch (start us, length us, event | category | flops | bytes accessed | tf_op | source)
XLA Modules:
  0.0 359.9 jit_solution(14492957873464296734)
XLA Ops:
  2.1 2.7 convolution_convert_fusion.3.q_ref.refs_0_
  6.1 1.5 convolution_convert_fusion.1.v_ref.refs_2_
  7.6 1.5 convolution_convert_fusion.g_ref.refs_3_
  10.2 13.7 %forward.1 = (bf16[256,1024]{1,0:T(8,128)(2,1)}, f32[256,1024]{1,0:T(8,128)}, f32[1,8,128,128]{3,2,1,0:T(8,128)}, f32[256,1024]{1,0:T(8,128)}, f32[256,1024]{1,0:T(8,128)}) custom-call(bf16[256,512]{1,0:T(8,128)(2,1)} %convolution_convert_fusion.3.q_ref.refs_0_, bf16[256,512]{1,0:T(8,128)(2,1)} %convolution_convert_fusion.2.k_ref.refs_1_, ...), custom_call_target="tpu_custom_call" | custom-call | tf_op jit(solution)/shard_map/forward/pallas_call | solution.py:349
  23.9 3.5 fusion.67
  27.4 3.0 collective-permute-start
  33.9 3.4 fusion.32
  37.3 16.6 %collective-permute-done = f32[256,1024]{1,0:T(8,128)} collective-permute-done((f32[256,1024]{1,0:T(8,128)}, f32[256,1024]{1,0:T(8,128)}, u32[]{:S(2)}, u32[]{:S(2)}) %collective-permute-start) | collective-permute-done | bytes 1048608 | tf_op jit(solution)/shard_map/ppermute | solution.py:442
  53.9 1.8 multiply_reduce_fusion.2
  57.9 3.9 %fusion.60 = (f32[256,1408]{1,0:T(8,128)}, bf16[256,1408]{1,0:T(8,128)(2,1)S(1)}, f32[256,1408]{1,0:T(8,128)}, bf16[256,1408]{1,0:T(8,128)(2,1)S(1)}, f32[256,1408]{1,0:T(8,128)}, /*index=5*/bf16[256,1408]{1,0:T(8,128)(2,1)}) fusion(f32[256,1408]{1,0:T(8,128)S(1)} %fusion.32, f32[256,1408]{1,0:T(8,128)S(1)} %fusion.68, ...), kind=kOutput, calls=%fused_computation.177 | convolution fusion | flops 745046016 | bytes 12779520 | tf_op jit(solution)/shard_map/dot_general | solution.py:623
  63.9 1.8 collective-permute-start.1
  67.8 2.0 fusion.50.refs_0_
  71.3 3.1 fusion.69
  77.0 13.2 %collective-permute-done.1 = f32[256,1024]{1,0:T(8,128)} collective-permute-done((f32[256,1024]{1,0:T(8,128)S(1)}, f32[256,1024]{1,0:T(8,128)}, u32[]{:S(2)}, u32[]{:S(2)}) %collective-permute-start.1) | collective-permute-done | bytes 1048608 | tf_op jit(solution)/shard_map/ppermute | solution.py:442
  90.2 1.5 multiply_reduce_fusion
  91.7 2.0 fusion.4
  93.8 17.0 %collective-permute-done.2 = f32[256,1024]{1,0:T(8,128)S(1)} collective-permute-done((f32[256,1024]{1,0:T(8,128)S(1)}, f32[256,1024]{1,0:T(8,128)S(1)}, u32[]{:S(2)}, u32[]{:S(2)}) %collective-permute-start.2) | collective-permute-done | bytes 1048608 | tf_op jit(solution)/shard_map/ppermute | solution.py:442
  110.8 1.8 fusion.27.refs_14_
  112.6 10.4 %shard_map.383 = (f32[256,1024]{1,0:T(8,128)}, f32[256,8]{1,0:T(8,128)}, f32[8,128]{1,0:T(8,128)}, f32[1,256]{1,0:T(1,128)}, f32[256,1536]{1,0:T(8,128)}, /*inde...) custom-call(bf16[256,512]{1,0:T(8,128)(2,1)} %convolution_convert_fusion.3.q_ref.refs_0_, ...), custom_call_target="tpu_custom_call" | custom-call | tf_op jit(solution)/shard_map/pallas_call | solution.py:422
  123.0 10.6 %shard_map.384 = (f32[256,1024]{1,0:T(8,128)}, f32[256,8]{1,0:T(8,128)}, f32[8,128]{1,0:T(8,128)}, f32[1,256]{1,0:T(1,128)}, f32[256,1536]{1,0:T(8,128)}, /*inde...) custom-call(bf16[256,512]{1,0:T(8,128)(2,1)} %convolution_convert_fusion.3.q_ref.refs_0_, ...), custom_call_target="tpu_custom_call" | custom-call | tf_op jit(solution)/shard_map/pallas_call | solution.py:422
  133.7 2.7 multiply_bitcast_fusion
  136.9 1.5 collective-permute-start.3
  138.9 9.0 %shard_map.387 = f32[512,4224]{1,0:T(8,128)} custom-call(f32[1024,256]{1,0:T(8,128)} %copy-done.20, f32[512,256]{1,0:T(8,128)} %collective-permute-done.42.refs_1_, f32[1024,256]{1,0:T(8,128)} %copy-done.19, f32[512,256]{1,0:T(8,128)} %collective-permute-done.43.refs_3_, bf16[256,1408]{1,0:T(8,128)(2,1)} %copy-done.30, bf16[256,1408]{1,0:T(8,128)(2,1)} %copy-done.18, ...), custom_call_target="tpu_custom_call" | custom-call | tf_op jit(solution)/shard_map/pallas_call | solution.py:553
  148.0 2.3 fusion.62
  152.8 9.5 %collective-permute-done.4 = f32[1,256]{1,0:T(1,128)S(1)} collective-permute-done((f32[1,256]{1,0:T(1,128)S(1)}, f32[1,256]{1,0:T(1,128)S(1)}, u32[]{:S(2)}, u32[]{:S(2)}) %collective-permute-start.4) | collective-permute-done | bytes 1056 | tf_op jit(solution)/shard_map/ppermute | solution.py:442
  162.3 2.0 fusion.3
  165.8 1.9 fusion.25.refs_2_
  170.1 2.7 slice_add_fusion.6
  173.6 1.5 collective-permute-start.7
  175.2 14.0 %collective-permute-done.7 = f32[154,128]{1,0:T(8,128)S(1)} collective-permute-done((f32[154,128]{1,0:T(8,128)S(1)}, f32[154,128]{1,0:T(8,128)S(1)}, u32[]{:S(2)}, u32[]{:S(2)}) %collective-permute-start.7) | collective-permute-done | bytes 78880 | tf_op jit(solution)/shard_map/ppermute | solution.py:451
  189.2 2.9 collective-permute-start.8
  192.0 2.6 fusion.6
  198.4 10.1 %collective-permute-done.48 = f32[32,4224]{1,0:T(8,128)S(1)} collective-permute-done((f32[32,4224]{1,0:T(8,128)}, f32[32,4224]{1,0:T(8,128)S(1)}, u32[]{:S(2)}, u32[]{:S(2)}) %collective-permute-start.48) | collective-permute-done | bytes 540704 | tf_op jit(solution)/shard_map/ppermute | solution.py:505
  209.3 2.5 slice_add_fusion.5
  211.9 2.0 collective-permute-start.49
  214.7 6.7 %shard_map.386 = f32[512,2048]{1,0:T(8,128)} custom-call(f32[1024,256]{1,0:T(8,128)} %copy-done.13, f32[512,256]{1,0:T(8,128)} %copy-done.21, f32[1024,256]{1,0:T(8,128)} %copy-done.14, f32[512,256]{1,0:T(8,128)} %copy-done.22, f32[256,1536]{1,0:T(8,128)} %get-tuple-element.67.refs_4_, bf16[256,1024]{1,0:T(8,128)(2,1)} %get-tuple-element.44.refs_5_, ...), custom_call_target="tpu_custom_call" | custom-call | tf_op jit(solution)/shard_map/pallas_call | solution.py:553
  222.9 1.7 collective-permute-start.35
  225.8 6.7 %shard_map.385 = f32[512,2048]{1,0:T(8,128)} custom-call(f32[1024,256]{1,0:T(8,128)} %copy-done.13, f32[512,256]{1,0:T(8,128)} %copy-done.21, f32[1024,256]{1,0:T(8,128)} %copy-done.14, f32[512,256]{1,0:T(8,128)} %copy-done.22, f32[256,1536]{1,0:T(8,128)} %get-tuple-element.65.refs_4_, bf16[256,1024]{1,0:T(8,128)(2,1)} %get-tuple-element.44.refs_5_, ...), custom_call_target="tpu_custom_call" | custom-call | tf_op jit(solution)/shard_map/pallas_call | solution.py:553
  234.1 1.7 collective-permute-start.20
  237.2 5.7 %collective-permute-done.13 = f32[32,2048]{1,0:T(8,128)S(1)} collective-permute-done((f32[32,2048]{1,0:T(8,128)S(1)}, f32[32,2048]{1,0:T(8,128)S(1)}, u32[]{:S(2)}, u32[]{:S(2)}) %collective-permute-start.13) | collective-permute-done | bytes 262176 | tf_op jit(solution)/shard_map/ppermute | solution.py:505
  244.1 2.0 collective-permute-start.14
  246.2 1.8 slice_add_fusion.4
  250.1 2.0 collective-permute-done.36
  252.6 1.6 collective-permute-done.14
  254.8 2.9 collective-permute-done.21
  258.2 13.2 %collective-permute-done.30 = f32[32,2048]{1,0:T(8,128)S(1)} collective-permute-done((f32[32,2048]{1,0:T(8,128)S(1)}, f32[32,2048]{1,0:T(8,128)S(1)}, u32[]{:S(2)}, u32[]{:S(2)}) %collective-permute-start.30) | collective-permute-done | bytes 262176 | tf_op jit(solution)/shard_map/ppermute | solution.py:505
  273.6 3.4 collective-permute-done.15
  279.1 2.1 collective-permute-start.16
  282.5 2.2 collective-permute-start.58
  284.7 1.5 collective-permute-done.38
  288.3 2.1 collective-permute-start.39
  293.1 12.4 %collective-permute-done.32 = f32[32,2048]{1,0:T(8,128)S(1)} collective-permute-done((f32[32,2048]{1,0:T(8,128)S(1)}, f32[32,2048]{1,0:T(8,128)S(1)}, u32[]{:S(2)}, u32[]{:S(2)}) %collective-permute-start.32) | collective-permute-done | bytes 262176 | tf_op jit(solution)/shard_map/ppermute | solution.py:505
  305.5 1.5 collective-permute-start.24
  307.5 2.2 collective-permute-start.33
  311.1 1.5 collective-permute-start.40
  313.5 2.7 collective-permute-start.18
  317.6 1.9 collective-permute-start.59
  320.4 1.5 collective-permute-start.34
  323.2 2.0 collective-permute-start.41
  326.0 1.5 collective-permute-start.19
  327.5 12.9 %collective-permute-done.34 = f32[32,2048]{1,0:T(8,128)S(1)} collective-permute-done((f32[32,2048]{1,0:T(8,128)S(1)}, f32[32,2048]{1,0:T(8,128)S(1)}, u32[]{:S(2)}, u32[]{:S(2)}) %collective-permute-start.34) | collective-permute-done | bytes 262176 | tf_op jit(solution)/shard_map/ppermute | solution.py:505
  343.9 2.2 collective-permute-start.60
  346.1 3.5 collective-permute-done.26
  352.0 5.5 %collective-permute-done.60 = f32[32,4224]{1,0:T(8,128)S(1)} collective-permute-done((f32[32,4224]{1,0:T(8,128)S(1)}, f32[32,4224]{1,0:T(8,128)S(1)}, u32[]{:S(2)}, u32[]{:S(2)}) %collective-permute-start.60) | collective-permute-done | bytes 540704 | tf_op jit(solution)/shard_map/ppermute | solution.py:506
  (270 shorter events, 65.6 us)
Async XLA Ops:
  0.7 57.2 %copy-start = (bf16[1024,1408]{1,0:T(8,128)(2,1)S(1)}, bf16[1024,1408]{1,0:T(8,128)(2,1)}, u32[]{:S(2)}) copy-start(bf16[1024,1408]{1,0:T(8,128)(2,1)} %param.42) | copy-start | bytes 8650756
  27.4 26.5 %collective-permute-start = (f32[256,1024]{1,0:T(8,128)}, f32[256,1024]{1,0:T(8,128)}, u32[]{:S(2)}, u32[]{:S(2)}) collective-permute-start(f32[256,1024]{1,0:T(8,128)} %fusion.67), channel_id=1, source_target_pairs={{0,1},{1,0},{2,3},{3,2},{4,5},{5,4},{6,7},{7,6},{8,9},{9,8},{10,11... | collective-permute-start | bytes 3145736 | tf_op jit(solution)/shard_map/ppermute | solution.py:442
  33.9 31.9 %copy-start.33 = (pred[512,1024]{1,0:T(32,128)(4,1)}, pred[512,1024]{1,0:T(32,128)(4,1)S(1)}, u32[]{:S(2)}) copy-start(pred[512,1024]{1,0:T(32,128)(4,1)S(1)} %get-tuple-element.153) | copy-start | bytes 1572868
  33.9 31.9 %copy-start.35 = (pred[512,1024]{1,0:T(32,128)(4,1)}, pred[512,1024]{1,0:T(32,128)(4,1)S(1)}, u32[]{:S(2)}) copy-start(pred[512,1024]{1,0:T(32,128)(4,1)S(1)} %get-tuple-element.154) | copy-start | bytes 1572868
  63.9 26.2 %collective-permute-start.1 = (f32[256,1024]{1,0:T(8,128)S(1)}, f32[256,1024]{1,0:T(8,128)}, u32[]{:S(2)}, u32[]{:S(2)}) collective-permute-start(f32[256,1024]{1,0:T(8,128)S(1)} %convolution_add_fusion), channel_id=1, source_target_pairs={{0,1},{1,0},{2,3},{3,2},{4,5},{5,4},{6,7},{7,6},{8,9},{9,8},{10,11... | collective-permute-start | bytes 3145736 | tf_op jit(solution)/shard_map/ppermute | solution.py:442
  67.5 68.8 %collective-permute-start.43 = (f32[512,256]{1,0:T(8,128)}, f32[512,256]{1,0:T(8,128)}, u32[]{:S(2)}, u32[]{:S(2)}) collective-permute-start(f32[512,256]{1,0:T(8,128)} %slice.400), channel_id=1, source_target_pairs={{0,2},{2,0},{4,6},{6,4},{8,10},{10,8},{12,14},{14,12},{16,18},{18,... | collective-permute-start | bytes 1572872 | tf_op jit(solution)/shard_map/ppermute | solution.py:442
  74.5 36.3 %collective-permute-start.2 = (f32[256,1024]{1,0:T(8,128)S(1)}, f32[256,1024]{1,0:T(8,128)S(1)}, u32[]{:S(2)}, u32[]{:S(2)}) collective-permute-start(f32[256,1024]{1,0:T(8,128)S(1)} %fusion.69), channel_id=1, source_target_pairs={{0,1},{1,0},{2,3},{3,2},{4,5},{5,4},{6,7},{7,6},{8,9},{9,8},{10,11... | collective-permute-start | bytes 3145736 | tf_op jit(solution)/shard_map/ppermute | solution.py:442
  76.5 61.8 %collective-permute-start.44 = (f32[256,1408]{1,0:T(8,128)}, f32[256,1408]{1,0:T(8,128)}, u32[]{:S(2)}, u32[]{:S(2)}) collective-permute-start(f32[256,1408]{1,0:T(8,128)} %get-tuple-element.128), channel_id=1, source_target_pairs={{0,2},{2,0},{4,6},{6,4},{8,10},{10,8},{12,14},{14,12},{16,18},{18,... | collective-permute-start | bytes 4325384 | tf_op jit(solution)/shard_map/ppermute | solution.py:442
  76.6 62.3 %collective-permute-start.45 = (f32[256,1408]{1,0:T(8,128)}, f32[256,1408]{1,0:T(8,128)}, u32[]{:S(2)}, u32[]{:S(2)}) collective-permute-start(f32[256,1408]{1,0:T(8,128)} %get-tuple-element.74), channel_id=1, source_target_pairs={{0,2},{2,0},{4,6},{6,4},{8,10},{10,8},{12,14},{14,12},{16,18},{18,... | collective-permute-start | bytes 4325384 | tf_op jit(solution)/shard_map/ppermute | solution.py:442
  90.1 48.7 %collective-permute-start.46 = (f32[256,1408]{1,0:T(8,128)}, f32[256,1408]{1,0:T(8,128)}, u32[]{:S(2)}, u32[]{:S(2)}) collective-permute-start(f32[256,1408]{1,0:T(8,128)} %get-tuple-element.130), channel_id=1, source_target_pairs={{0,2},{2,0},{4,6},{6,4},{8,10},{10,8},{12,14},{14,12},{16,18},{18,... | collective-permute-start | bytes 4325384 | tf_op jit(solution)/shard_map/ppermute | solution.py:442
  110.8 26.0 %collective-permute-start.42 = (f32[512,256]{1,0:T(8,128)}, f32[512,256]{1,0:T(8,128)}, u32[]{:S(2)}, u32[]{:S(2)}) collective-permute-start(f32[512,256]{1,0:T(8,128)} %slice.399), channel_id=1, source_target_pairs={{0,2},{2,0},{4,6},{6,4},{8,10},{10,8},{12,14},{14,12},{16,18},{18,... | collective-permute-start | bytes 1572872 | tf_op jit(solution)/shard_map/ppermute | solution.py:442
  136.3 75.5 %collective-permute-start.9 = (f32[512,256]{1,0:T(8,128)}, f32[512,256]{1,0:T(8,128)S(1)}, u32[]{:S(2)}, u32[]{:S(2)}) collective-permute-start(f32[512,256]{1,0:T(8,128)} %slice.354), channel_id=1, source_target_pairs={{0,2},{2,0},{4,6},{6,4},{8,10},{10,8},{12,14},{14,12},{16,18},{18,... | collective-permute-start | bytes 1572872 | tf_op jit(solution)/shard_map/ppermute | solution.py:442
  136.9 25.4 %collective-permute-start.3 = (f32[256,1024]{1,0:T(8,128)}, f32[256,1024]{1,0:T(8,128)S(1)}, u32[]{:S(2)}, u32[]{:S(2)}) collective-permute-start(f32[256,1024]{1,0:T(8,128)} %get-tuple-element.55), channel_id=1, source_target_pairs={{0,1},{1,0},{2,3},{3,2},{4,5},{5,4},{6,7},{7,6},{8,9},{9,8},{10,11... | collective-permute-start | bytes 3145736 | tf_op jit(solution)/shard_map/ppermute | solution.py:442
  138.3 23.9 %collective-permute-start.4 = (f32[1,256]{1,0:T(1,128)S(1)}, f32[1,256]{1,0:T(1,128)S(1)}, u32[]{:S(2)}, u32[]{:S(2)}) collective-permute-start(f32[1,256]{1,0:T(1,128)S(1)} %copy-done.48), channel_id=1, source_target_pairs={{0,1},{1,0},{2,3},{3,2},{4,5},{5,4},{6,7},{7,6},{8,9},{9,8},{10,11... | collective-permute-start | bytes 3080 | tf_op jit(solution)/shard_map/ppermute | solution.py:442
  150.3 18.4 %collective-permute-start.54 = (f32[32,4224]{1,0:T(8,128)}, f32[32,4224]{1,0:T(8,128)}, u32[]{:S(2)}, u32[]{:S(2)}) collective-permute-start(f32[32,4224]{1,0:T(8,128)} %get-tuple-element.94), channel_id=1, source_target_pairs={{8,0},{10,2},{16,8},{18,10},{24,16},{26,18},{28,24},{30,26},{20,28... | collective-permute-start | bytes 1622024 | tf_op jit(solution)/shard_map/ppermute | solution.py:506
  151.7 18.4 %collective-permute-start.47 = (f32[32,4224]{1,0:T(8,128)}, f32[32,4224]{1,0:T(8,128)}, u32[]{:S(2)}, u32[]{:S(2)}) collective-permute-start(f32[32,4224]{1,0:T(8,128)} %get-tuple-element.95), channel_id=1, source_target_pairs={{0,8},{2,10},{8,16},{10,18},{16,24},{18,26},{24,28},{26,30},{28,20... | collective-permute-start | bytes 1622024 | tf_op jit(solution)/shard_map/ppermute | solution.py:505
  162.3 49.6 %collective-permute-start.12 = (f32[256,1024]{1,0:T(8,128)}, f32[256,1024]{1,0:T(8,128)}, u32[]{:S(2)}, u32[]{:S(2)}) collective-permute-start(f32[256,1024]{1,0:T(8,128)} %get-tuple-element.66), channel_id=1, source_target_pairs={{0,2},{2,0},{4,6},{6,4},{8,10},{10,8},{12,14},{14,12},{16,18},{18,... | collective-permute-start | bytes 3145736 | tf_op jit(solution)/shard_map/ppermute | solution.py:442
  165.2 3.4 collective-permute-start.5
  168.6 45.3 %collective-permute-start.27 = (f32[256,1536]{1,0:T(8,128)}, f32[256,1536]{1,0:T(8,128)}, u32[]{:S(2)}, u32[]{:S(2)}) collective-permute-start(f32[256,1536]{1,0:T(8,128)} %get-tuple-element.67.refs_4_), channel_id=1, source_target_pairs={{0,2},{2,0},{4,6},{6,4},{8,10},{10,8},{12,14},{14,12},{16,18},{18,... | collective-permute-start | bytes 4718600 | tf_op jit(solution)/shard_map/ppermute | solution.py:442
  168.7 4.9 %collective-permute-start.6 = (f32[154,128]{1,0:T(8,128)S(1)}, f32[154,128]{1,0:T(8,128)S(1)}, u32[]{:S(2)}, u32[]{:S(2)}) collective-permute-start(f32[154,128]{1,0:T(8,128)S(1)} %add.271), channel_id=1, source_target_pairs={{0,4},{2,6},{4,0},{6,2},{8,12},{10,14},{12,8},{14,10},{16,20},{18,... | collective-permute-start | bytes 236552 | tf_op jit(solution)/shard_map/ppermute | solution.py:451
  172.8 25.6 %collective-permute-start.55 = (f32[32,4224]{1,0:T(8,128)}, f32[32,4224]{1,0:T(8,128)S(1)}, u32[]{:S(2)}, u32[]{:S(2)}) collective-permute-start(f32[32,4224]{1,0:T(8,128)} %get-tuple-element.92), channel_id=1, source_target_pairs={{8,0},{10,2},{16,8},{18,10},{24,16},{26,18},{28,24},{30,26},{20,28... | collective-permute-start | bytes 1622024 | tf_op jit(solution)/shard_map/ppermute | solution.py:506
  173.6 15.5 %collective-permute-start.7 = (f32[154,128]{1,0:T(8,128)S(1)}, f32[154,128]{1,0:T(8,128)S(1)}, u32[]{:S(2)}, u32[]{:S(2)}) collective-permute-start(f32[154,128]{1,0:T(8,128)S(1)} %add.272), channel_id=1, source_target_pairs={{0,8},{2,10},{4,12},{6,14},{8,0},{10,2},{12,4},{14,6},{16,24},{18,... | collective-permute-start | bytes 236552 | tf_op jit(solution)/shard_map/ppermute | solution.py:451
  189.2 5.6 %collective-permute-start.8 = (f32[154,128]{1,0:T(8,128)S(1)}, f32[154,128]{1,0:T(8,128)S(1)}, u32[]{:S(2)}, u32[]{:S(2)}) collective-permute-start(f32[154,128]{1,0:T(8,128)S(1)} %add.273), channel_id=1, source_target_pairs={{0,16},{2,18},{4,20},{6,22},{8,24},{10,26},{12,28},{14,30},{16,0},... | collective-permute-start | bytes 236552 | tf_op jit(solution)/shard_map/ppermute | solution.py:451
  194.7 13.8 %collective-permute-start.48 = (f32[32,4224]{1,0:T(8,128)}, f32[32,4224]{1,0:T(8,128)S(1)}, u32[]{:S(2)}, u32[]{:S(2)}) collective-permute-start(f32[32,4224]{1,0:T(8,128)} %get-tuple-element.93), channel_id=1, source_target_pairs={{0,8},{2,10},{8,16},{10,18},{16,24},{18,26},{24,28},{26,30},{28,20... | collective-permute-start | bytes 1622024 | tf_op jit(solution)/shard_map/ppermute | solution.py:505
  198.4 15.5 %collective-permute-start.10 = (f32[512,256]{1,0:T(8,128)}, f32[512,256]{1,0:T(8,128)S(1)}, u32[]{:S(2)}, u32[]{:S(2)}) collective-permute-start(f32[512,256]{1,0:T(8,128)} %slice.355), channel_id=1, source_target_pairs={{0,2},{2,0},{4,6},{6,4},{8,10},{10,8},{12,14},{14,12},{16,18},{18,... | collective-permute-start | bytes 1572872 | tf_op jit(solution)/shard_map/ppermute | solution.py:442
  209.3 15.3 %collective-permute-start.11 = (f32[256,1536]{1,0:T(8,128)}, f32[256,1536]{1,0:T(8,128)S(1)}, u32[]{:S(2)}, u32[]{:S(2)}) collective-permute-start(f32[256,1536]{1,0:T(8,128)} %get-tuple-element.65.refs_4_), channel_id=1, source_target_pairs={{0,2},{2,0},{4,6},{6,4},{8,10},{10,8},{12,14},{14,12},{16,18},{18,... | collective-permute-start | bytes 4718600 | tf_op jit(solution)/shard_map/ppermute | solution.py:442
  211.9 34.3 %collective-permute-start.56 = (f32[32,4224]{1,0:T(8,128)}, f32[32,4224]{1,0:T(8,128)}, u32[]{:S(2)}, u32[]{:S(2)}) collective-permute-start(f32[32,4224]{1,0:T(8,128)} %get-tuple-element.90), channel_id=1, source_target_pairs={{8,0},{10,2},{16,8},{18,10},{24,16},{26,18},{28,24},{30,26},{20,28... | collective-permute-start | bytes 1622024 | tf_op jit(solution)/shard_map/ppermute | solution.py:506
  211.9 34.3 %collective-permute-start.49 = (f32[32,4224]{1,0:T(8,128)S(1)}, f32[32,4224]{1,0:T(8,128)}, u32[]{:S(2)}, u32[]{:S(2)}) collective-permute-start(f32[32,4224]{1,0:T(8,128)S(1)} %get-tuple-element.91), channel_id=1, source_target_pairs={{0,8},{2,10},{8,16},{10,18},{16,24},{18,26},{24,28},{26,30},{28,20... | collective-permute-start | bytes 1622024 | tf_op jit(solution)/shard_map/ppermute | solution.py:505
  222.5 11.5 %collective-permute-start.28 = (f32[32,2048]{1,0:T(8,128)S(1)}, f32[32,2048]{1,0:T(8,128)S(1)}, u32[]{:S(2)}, u32[]{:S(2)}) collective-permute-start(f32[32,2048]{1,0:T(8,128)S(1)} %get-tuple-element.126), channel_id=1, source_target_pairs={{0,8},{2,10},{8,16},{10,18},{16,24},{18,26},{24,28},{26,30},{28,20... | collective-permute-start | bytes 786440 | tf_op jit(solution)/shard_map/ppermute | solution.py:505
  222.9 12.9 %collective-permute-start.35 = (f32[32,2048]{1,0:T(8,128)S(1)}, f32[32,2048]{1,0:T(8,128)S(1)}, u32[]{:S(2)}, u32[]{:S(2)}) collective-permute-start(f32[32,2048]{1,0:T(8,128)S(1)} %get-tuple-element.127), channel_id=1, source_target_pairs={{8,0},{10,2},{16,8},{18,10},{24,16},{26,18},{28,24},{30,26},{20,28... | collective-permute-start | bytes 786440 | tf_op jit(solution)/shard_map/ppermute | solution.py:506
  233.7 9.2 %collective-permute-start.13 = (f32[32,2048]{1,0:T(8,128)S(1)}, f32[32,2048]{1,0:T(8,128)S(1)}, u32[]{:S(2)}, u32[]{:S(2)}) collective-permute-start(f32[32,2048]{1,0:T(8,128)S(1)} %get-tuple-element.110), channel_id=1, source_target_pairs={{0,8},{2,10},{8,16},{10,18},{16,24},{18,26},{24,28},{26,30},{28,20... | collective-permute-start | bytes 786440 | tf_op jit(solution)/shard_map/ppermute | solution.py:505
  234.1 9.0 %collective-permute-start.20 = (f32[32,2048]{1,0:T(8,128)S(1)}, f32[32,2048]{1,0:T(8,128)S(1)}, u32[]{:S(2)}, u32[]{:S(2)}) collective-permute-start(f32[32,2048]{1,0:T(8,128)S(1)} %get-tuple-element.111), channel_id=1, source_target_pairs={{8,0},{10,2},{16,8},{18,10},{24,16},{26,18},{28,24},{30,26},{20,28... | collective-permute-start | bytes 786440 | tf_op jit(solution)/shard_map/ppermute | solution.py:506
  236.9 12.5 %collective-permute-start.29 = (f32[32,2048]{1,0:T(8,128)S(1)}, f32[32,2048]{1,0:T(8,128)S(1)}, u32[]{:S(2)}, u32[]{:S(2)}) collective-permute-start(f32[32,2048]{1,0:T(8,128)S(1)} %get-tuple-element.124), channel_id=1, source_target_pairs={{0,8},{2,10},{8,16},{10,18},{16,24},{18,26},{24,28},{26,30},{28,20... | collective-permute-start | bytes 786440 | tf_op jit(solution)/shard_map/ppermute | solution.py:505
  243.0 9.2 %collective-permute-start.36 = (f32[32,2048]{1,0:T(8,128)S(1)}, f32[32,2048]{1,0:T(8,128)S(1)}, u32[]{:S(2)}, u32[]{:S(2)}) collective-permute-start(f32[32,2048]{1,0:T(8,128)S(1)} %get-tuple-element.125), channel_id=1, source_target_pairs={{8,0},{10,2},{16,8},{18,10},{24,16},{26,18},{28,24},{30,26},{20,28... | collective-permute-start | bytes 786440 | tf_op jit(solution)/shard_map/ppermute | solution.py:506
  244.1 10.1 %collective-permute-start.14 = (f32[32,2048]{1,0:T(8,128)S(1)}, f32[32,2048]{1,0:T(8,128)S(1)}, u32[]{:S(2)}, u32[]{:S(2)}) collective-permute-start(f32[32,2048]{1,0:T(8,128)S(1)} %get-tuple-element.108), channel_id=1, source_target_pairs={{0,8},{2,10},{8,16},{10,18},{16,24},{18,26},{24,28},{26,30},{28,20... | collective-permute-start | bytes 786440 | tf_op jit(solution)/shard_map/ppermute | solution.py:505
  246.1 11.6 %collective-permute-start.21 = (f32[32,2048]{1,0:T(8,128)S(1)}, f32[32,2048]{1,0:T(8,128)S(1)}, u32[]{:S(2)}, u32[]{:S(2)}) collective-permute-start(f32[32,2048]{1,0:T(8,128)S(1)} %get-tuple-element.109), channel_id=1, source_target_pairs={{8,0},{10,2},{16,8},{18,10},{24,16},{26,18},{28,24},{30,26},{20,28... | collective-permute-start | bytes 786440 | tf_op jit(solution)/shard_map/ppermute | solution.py:506
  248.0 33.1 %collective-permute-start.57 = (f32[32,4224]{1,0:T(8,128)S(1)}, f32[32,4224]{1,0:T(8,128)S(1)}, u32[]{:S(2)}, u32[]{:S(2)}) collective-permute-start(f32[32,4224]{1,0:T(8,128)S(1)} %get-tuple-element.88), channel_id=1, source_target_pairs={{8,0},{10,2},{16,8},{18,10},{24,16},{26,18},{28,24},{30,26},{20,28... | collective-permute-start | bytes 1622024 | tf_op jit(solution)/shard_map/ppermute | solution.py:506
  249.4 31.8 %collective-permute-start.50 = (f32[32,4224]{1,0:T(8,128)S(1)}, f32[32,4224]{1,0:T(8,128)S(1)}, u32[]{:S(2)}, u32[]{:S(2)}) collective-permute-start(f32[32,4224]{1,0:T(8,128)S(1)} %get-tuple-element.89), channel_id=1, source_target_pairs={{0,8},{2,10},{8,16},{10,18},{16,24},{18,26},{24,28},{26,30},{28,20... | collective-permute-start | bytes 1622024 | tf_op jit(solution)/shard_map/ppermute | solution.py:505
  252.2 19.2 %collective-permute-start.30 = (f32[32,2048]{1,0:T(8,128)S(1)}, f32[32,2048]{1,0:T(8,128)S(1)}, u32[]{:S(2)}, u32[]{:S(2)}) collective-permute-start(f32[32,2048]{1,0:T(8,128)S(1)} %get-tuple-element.122), channel_id=1, source_target_pairs={{0,8},{2,10},{8,16},{10,18},{16,24},{18,26},{24,28},{26,30},{28,20... | collective-permute-start | bytes 786440 | tf_op jit(solution)/shard_map/ppermute | solution.py:505
  254.2 17.9 %collective-permute-start.37 = (f32[32,2048]{1,0:T(8,128)S(1)}, f32[32,2048]{1,0:T(8,128)S(1)}, u32[]{:S(2)}, u32[]{:S(2)}) collective-permute-start(f32[32,2048]{1,0:T(8,128)S(1)} %get-tuple-element.123), channel_id=1, source_target_pairs={{8,0},{10,2},{16,8},{18,10},{24,16},{26,18},{28,24},{30,26},{20,28... | collective-permute-start | bytes 786440 | tf_op jit(solution)/shard_map/ppermute | solution.py:506
  257.8 19.2 %collective-permute-start.15 = (f32[32,2048]{1,0:T(8,128)S(1)}, f32[32,2048]{1,0:T(8,128)S(1)}, u32[]{:S(2)}, u32[]{:S(2)}) collective-permute-start(f32[32,2048]{1,0:T(8,128)S(1)} %get-tuple-element.106), channel_id=1, source_target_pairs={{0,8},{2,10},{8,16},{10,18},{16,24},{18,26},{24,28},{26,30},{28,20... | collective-permute-start | bytes 786440 | tf_op jit(solution)/shard_map/ppermute | solution.py:505
  271.4 7.6 %collective-permute-start.22 = (f32[32,2048]{1,0:T(8,128)S(1)}, f32[32,2048]{1,0:T(8,128)S(1)}, u32[]{:S(2)}, u32[]{:S(2)}) collective-permute-start(f32[32,2048]{1,0:T(8,128)S(1)} %get-tuple-element.107), channel_id=1, source_target_pairs={{8,0},{10,2},{16,8},{18,10},{24,16},{26,18},{28,24},{30,26},{20,28... | collective-permute-start | bytes 786440 | tf_op jit(solution)/shard_map/ppermute | solution.py:506
  272.2 12.5 %collective-permute-start.31 = (f32[32,2048]{1,0:T(8,128)S(1)}, f32[32,2048]{1,0:T(8,128)S(1)}, u32[]{:S(2)}, u32[]{:S(2)}) collective-permute-start(f32[32,2048]{1,0:T(8,128)S(1)} %get-tuple-element.120), channel_id=1, source_target_pairs={{0,8},{2,10},{8,16},{10,18},{16,24},{18,26},{24,28},{26,30},{28,20... | collective-permute-start | bytes 786440 | tf_op jit(solution)/shard_map/ppermute | solution.py:505
  277.0 9.2 %collective-permute-start.38 = (f32[32,2048]{1,0:T(8,128)S(1)}, f32[32,2048]{1,0:T(8,128)S(1)}, u32[]{:S(2)}, u32[]{:S(2)}) collective-permute-start(f32[32,2048]{1,0:T(8,128)S(1)} %get-tuple-element.121), channel_id=1, source_target_pairs={{8,0},{10,2},{16,8},{18,10},{24,16},{26,18},{28,24},{30,26},{20,28... | collective-permute-start | bytes 786440 | tf_op jit(solution)/shard_map/ppermute | solution.py:506
  279.1 9.2 %collective-permute-start.16 = (f32[32,2048]{1,0:T(8,128)S(1)}, f32[32,2048]{1,0:T(8,128)S(1)}, u32[]{:S(2)}, u32[]{:S(2)}) collective-permute-start(f32[32,2048]{1,0:T(8,128)S(1)} %get-tuple-element.104), channel_id=1, source_target_pairs={{0,8},{2,10},{8,16},{10,18},{16,24},{18,26},{24,28},{26,30},{28,20... | collective-permute-start | bytes 786440 | tf_op jit(solution)/shard_map/ppermute | solution.py:505
  281.2 10.6 %collective-permute-start.23 = (f32[32,2048]{1,0:T(8,128)S(1)}, f32[32,2048]{1,0:T(8,128)S(1)}, u32[]{:S(2)}, u32[]{:S(2)}) collective-permute-start(f32[32,2048]{1,0:T(8,128)S(1)} %get-tuple-element.105), channel_id=1, source_target_pairs={{8,0},{10,2},{16,8},{18,10},{24,16},{26,18},{28,24},{30,26},{20,28... | collective-permute-start | bytes 786440 | tf_op jit(solution)/shard_map/ppermute | solution.py:506
  282.5 33.8 %collective-permute-start.58 = (f32[32,4224]{1,0:T(8,128)S(1)}, f32[32,4224]{1,0:T(8,128)S(1)}, u32[]{:S(2)}, u32[]{:S(2)}) collective-permute-start(f32[32,4224]{1,0:T(8,128)S(1)} %get-tuple-element.86), channel_id=1, source_target_pairs={{8,0},{10,2},{16,8},{18,10},{24,16},{26,18},{28,24},{30,26},{20,28... | collective-permute-start | bytes 1622024 | tf_op jit(solution)/shard_map/ppermute | solution.py:506
  284.7 31.6 %collective-permute-start.51 = (f32[32,4224]{1,0:T(8,128)S(1)}, f32[32,4224]{1,0:T(8,128)S(1)}, u32[]{:S(2)}, u32[]{:S(2)}) collective-permute-start(f32[32,4224]{1,0:T(8,128)S(1)} %get-tuple-element.87), channel_id=1, source_target_pairs={{0,8},{2,10},{8,16},{10,18},{16,24},{18,26},{24,28},{26,30},{28,20... | collective-permute-start | bytes 1622024 | tf_op jit(solution)/shard_map/ppermute | solution.py:505
  286.3 19.2 %collective-permute-start.32 = (f32[32,2048]{1,0:T(8,128)S(1)}, f32[32,2048]{1,0:T(8,128)S(1)}, u32[]{:S(2)}, u32[]{:S(2)}) collective-permute-start(f32[32,2048]{1,0:T(8,128)S(1)} %get-tuple-element.118), channel_id=1, source_target_pairs={{0,8},{2,10},{8,16},{10,18},{16,24},{18,26},{24,28},{26,30},{28,20... | collective-permute-start | bytes 786440 | tf_op jit(solution)/shard_map/ppermute | solution.py:505
  288.3 19.2 %collective-permute-start.39 = (f32[32,2048]{1,0:T(8,128)S(1)}, f32[32,2048]{1,0:T(8,128)S(1)}, u32[]{:S(2)}, u32[]{:S(2)}) collective-permute-start(f32[32,2048]{1,0:T(8,128)S(1)} %get-tuple-element.119), channel_id=1, source_target_pairs={{8,0},{10,2},{16,8},{18,10},{24,16},{26,18},{28,24},{30,26},{20,28... | collective-permute-start | bytes 786440 | tf_op jit(solution)/shard_map/ppermute | solution.py:506
  291.9 19.2 %collective-permute-start.17 = (f32[32,2048]{1,0:T(8,128)S(1)}, f32[32,2048]{1,0:T(8,128)S(1)}, u32[]{:S(2)}, u32[]{:S(2)}) collective-permute-start(f32[32,2048]{1,0:T(8,128)S(1)} %get-tuple-element.102), channel_id=1, source_target_pairs={{0,8},{2,10},{8,16},{10,18},{16,24},{18,26},{24,28},{26,30},{28,20... | collective-permute-start | bytes 786440 | tf_op jit(solution)/shard_map/ppermute | solution.py:505
  305.5 8.0 %collective-permute-start.24 = (f32[32,2048]{1,0:T(8,128)S(1)}, f32[32,2048]{1,0:T(8,128)S(1)}, u32[]{:S(2)}, u32[]{:S(2)}) collective-permute-start(f32[32,2048]{1,0:T(8,128)S(1)} %get-tuple-element.103), channel_id=1, source_target_pairs={{8,0},{10,2},{16,8},{18,10},{24,16},{26,18},{28,24},{30,26},{20,28... | collective-permute-start | bytes 786440 | tf_op jit(solution)/shard_map/ppermute | solution.py:506
  307.5 12.0 %collective-permute-start.33 = (f32[32,2048]{1,0:T(8,128)S(1)}, f32[32,2048]{1,0:T(8,128)S(1)}, u32[]{:S(2)}, u32[]{:S(2)}) collective-permute-start(f32[32,2048]{1,0:T(8,128)S(1)} %get-tuple-element.116), channel_id=1, source_target_pairs={{0,8},{2,10},{8,16},{10,18},{16,24},{18,26},{24,28},{26,30},{28,20... | collective-permute-start | bytes 786440 | tf_op jit(solution)/shard_map/ppermute | solution.py:505
  311.1 9.2 %collective-permute-start.40 = (f32[32,2048]{1,0:T(8,128)S(1)}, f32[32,2048]{1,0:T(8,128)S(1)}, u32[]{:S(2)}, u32[]{:S(2)}) collective-permute-start(f32[32,2048]{1,0:T(8,128)S(1)} %get-tuple-element.117), channel_id=1, source_target_pairs={{8,0},{10,2},{16,8},{18,10},{24,16},{26,18},{28,24},{30,26},{20,28... | collective-permute-start | bytes 786440 | tf_op jit(solution)/shard_map/ppermute | solution.py:506
  313.5 9.7 %collective-permute-start.18 = (f32[32,2048]{1,0:T(8,128)S(1)}, f32[32,2048]{1,0:T(8,128)S(1)}, u32[]{:S(2)}, u32[]{:S(2)}) collective-permute-start(f32[32,2048]{1,0:T(8,128)S(1)} %get-tuple-element.100), channel_id=1, source_target_pairs={{0,8},{2,10},{8,16},{10,18},{16,24},{18,26},{24,28},{26,30},{28,20... | collective-permute-start | bytes 786440 | tf_op jit(solution)/shard_map/ppermute | solution.py:505
  316.3 9.6 %collective-permute-start.25 = (f32[32,2048]{1,0:T(8,128)S(1)}, f32[32,2048]{1,0:T(8,128)S(1)}, u32[]{:S(2)}, u32[]{:S(2)}) collective-permute-start(f32[32,2048]{1,0:T(8,128)S(1)} %get-tuple-element.101), channel_id=1, source_target_pairs={{8,0},{10,2},{16,8},{18,10},{24,16},{26,18},{28,24},{30,26},{20,28... | collective-permute-start | bytes 786440 | tf_op jit(solution)/shard_map/ppermute | solution.py:506
  317.6 24.9 %collective-permute-start.59 = (f32[32,4224]{1,0:T(8,128)S(1)}, f32[32,4224]{1,0:T(8,128)S(1)}, u32[]{:S(2)}, u32[]{:S(2)}) collective-permute-start(f32[32,4224]{1,0:T(8,128)S(1)} %get-tuple-element.84), channel_id=1, source_target_pairs={{8,0},{10,2},{16,8},{18,10},{24,16},{26,18},{28,24},{30,26},{20,28... | collective-permute-start | bytes 1622024 | tf_op jit(solution)/shard_map/ppermute | solution.py:506
  319.5 23.1 %collective-permute-start.52 = (f32[32,4224]{1,0:T(8,128)S(1)}, f32[32,4224]{1,0:T(8,128)S(1)}, u32[]{:S(2)}, u32[]{:S(2)}) collective-permute-start(f32[32,4224]{1,0:T(8,128)S(1)} %get-tuple-element.85), channel_id=1, source_target_pairs={{0,8},{2,10},{8,16},{10,18},{16,24},{18,26},{24,28},{26,30},{28,20... | collective-permute-start | bytes 1622024 | tf_op jit(solution)/shard_map/ppermute | solution.py:505
  320.4 20.1 %collective-permute-start.34 = (f32[32,2048]{1,0:T(8,128)S(1)}, f32[32,2048]{1,0:T(8,128)S(1)}, u32[]{:S(2)}, u32[]{:S(2)}) collective-permute-start(f32[32,2048]{1,0:T(8,128)S(1)} %get-tuple-element.114), channel_id=1, source_target_pairs={{0,8},{2,10},{8,16},{10,18},{16,24},{18,26},{24,28},{26,30},{28,20... | collective-permute-start | bytes 786440 | tf_op jit(solution)/shard_map/ppermute | solution.py:505
  323.2 19.2 %collective-permute-start.41 = (f32[32,2048]{1,0:T(8,128)S(1)}, f32[32,2048]{1,0:T(8,128)S(1)}, u32[]{:S(2)}, u32[]{:S(2)}) collective-permute-start(f32[32,2048]{1,0:T(8,128)S(1)} %get-tuple-element.115), channel_id=1, source_target_pairs={{8,0},{10,2},{16,8},{18,10},{24,16},{26,18},{28,24},{30,26},{20,28... | collective-permute-start | bytes 786440 | tf_op jit(solution)/shard_map/ppermute | solution.py:506
  326.0 20.2 %collective-permute-start.19 = (f32[32,2048]{1,0:T(8,128)S(1)}, f32[32,2048]{1,0:T(8,128)S(1)}, u32[]{:S(2)}, u32[]{:S(2)}) collective-permute-start(f32[32,2048]{1,0:T(8,128)S(1)} %get-tuple-element.98), channel_id=1, source_target_pairs={{0,8},{2,10},{8,16},{10,18},{16,24},{18,26},{24,28},{26,30},{28,20... | collective-permute-start | bytes 786440 | tf_op jit(solution)/shard_map/ppermute | solution.py:505
  340.4 9.2 %collective-permute-start.26 = (f32[32,2048]{1,0:T(8,128)S(1)}, f32[32,2048]{1,0:T(8,128)S(1)}, u32[]{:S(2)}, u32[]{:S(2)}) collective-permute-start(f32[32,2048]{1,0:T(8,128)S(1)} %get-tuple-element.99), channel_id=1, source_target_pairs={{8,0},{10,2},{16,8},{18,10},{24,16},{26,18},{28,24},{30,26},{20,28... | collective-permute-start | bytes 786440 | tf_op jit(solution)/shard_map/ppermute | solution.py:506
  343.9 13.6 %collective-permute-start.60 = (f32[32,4224]{1,0:T(8,128)S(1)}, f32[32,4224]{1,0:T(8,128)S(1)}, u32[]{:S(2)}, u32[]{:S(2)}) collective-permute-start(f32[32,4224]{1,0:T(8,128)S(1)} %get-tuple-element.82), channel_id=1, source_target_pairs={{8,0},{10,2},{16,8},{18,10},{24,16},{26,18},{28,24},{30,26},{20,28... | collective-permute-start | bytes 1622024 | tf_op jit(solution)/shard_map/ppermute | solution.py:506
  346.1 11.4 %collective-permute-start.53 = (f32[32,4224]{1,0:T(8,128)S(1)}, f32[32,4224]{1,0:T(8,128)S(1)}, u32[]{:S(2)}, u32[]{:S(2)}) collective-permute-start(f32[32,4224]{1,0:T(8,128)S(1)} %get-tuple-element.83), channel_id=1, source_target_pairs={{0,8},{2,10},{8,16},{10,18},{16,24},{18,26},{24,28},{26,30},{28,20... | collective-permute-start | bytes 1622024 | tf_op jit(solution)/shard_map/ppermute | solution.py:505
  (49 other events, 336.7 us)
